TPU v7x, 512 devices: a whole 4x8x8 slice. The times are simulated.
512 devices in a mesh: gx: 8 (over x, core), gy: 8 (over y), obs: 8 (over z).
Axes of the slice: x: 4, y: 8, z: 8, core: 2. Of those that a mesh axis runs over, the one named last changes fastest.
Arguments:
- control: float32 [4, 8, 1024, 1024], P(None, 'obs', 'gy', 'gx'), may hold values from -6 to 6
- diffusivity: float32 [2, 8, 1024, 1024], P(None, 'obs', 'gy', 'gx'), may hold values from 0.12 to 0.245
- prof_tile: int32 [32768, 1], P(('gx', 'gy')), may hold values from 0 to 63; in each aligned block of 512 rows (0 to 511, 512 to 1023, ...) at most 16 rows name the same one
- prof_cell: int32 [32768], P(('gx', 'gy')), may hold values from 0 to 16383
- obs_prof: int32 [262144], P(('gx', 'gy', 'obs')), may hold values from 0 to 511
- obs_field: int32 [262144], P(('gx', 'gy', 'obs')), may hold values from 0 to 3
- obs_level: int32 [262144], P(('gx', 'gy', 'obs')), may hold values from 0 to 6
- obs_weight: float32 [262144], P(('gx', 'gy', 'obs')), may hold values from 0 to 1
- innovation: float32 [262144], P(('gx', 'gy', 'obs')), may hold values from -6 to 6
- obs_precision: float32 [262144], P(('gx', 'gy', 'obs')), may hold values from 0.25 to 4
Outputs:
- gradient: float32 [4, 8, 1024, 1024], P(None, 'obs', 'gy', 'gx')
- departures: float32 [262144], P(('gx', 'gy', 'obs'))
Inputs may be any that keep to these rules, and one draw needn't show every extreme that they name: `prof_tile`: in each aligned block of 512 rows (the profiles of one tile) no tile is named by more than 16 rows; in some blocks one tile is named by exactly 16 rows.
All inputs are finite; a program needn't handle non-finite values.
Results may differ from a plain program's by a relative error of at most 0.00002.
Values sent between devices are 32-bit elements; how exact they have to be, the bound alone decides.
No kernel may reach another device: no remote copies, remote signals or barrier semaphores. Data moves between devices by JAX's collectives and lax.ppermute only.
A program may use at most 64 MiB of HBM per device.

v0:
```python
import jax
import jax.numpy as jnp
from jax import lax
from jax.sharding import PartitionSpec as P

STEPS = 10


def passed_along(value, axis, by):
    length = lax.axis_size(axis)
    return lax.ppermute(value, axis, [(i, (i + by) % length) for i in range(length)])


def shifted(block, axis, distance):
    devices = range(lax.axis_size(axis))
    route = [(i - distance, i) for i in devices if i - distance in devices]
    return lax.ppermute(block, axis, route)


def with_halo(block, sides, width):
    for axis, dim in sides:
        count = lax.axis_size(axis)
        forward = [(i, i + 1) for i in range(count - 1)]
        forward.append((count - 1, 0))
        backward = [(target, source) for source, target in forward]
        low = lax.ppermute(
            lax.slice_in_dim(block, block.shape[dim] - width, None, axis=dim), axis, forward
        )
        high = lax.ppermute(lax.slice_in_dim(block, 0, width, axis=dim), axis, backward)
        block = jnp.concatenate([low, block, high], axis=dim)
    return block


def advance(padded, east_rate, north_rate):
    center = padded[:, :, 1:-1, 1:-1]
    east_flux = east_rate[:, 1:-1, 1:-1] * (padded[:, :, 1:-1, 2:] - center)
    west_flux = east_rate[:, 1:-1, :-2] * (padded[:, :, 1:-1, :-2] - center)
    north_flux = north_rate[:, 1:-1, 1:-1] * (padded[:, :, 2:, 1:-1] - center)
    south_flux = north_rate[:, :-2, 1:-1] * (padded[:, :, :-2, 1:-1] - center)
    return center + east_flux + west_flux + north_flux + south_flux


def per_device(
    control,
    diffusivity,
    prof_tile,
    prof_cell,
    obs_prof,
    obs_field,
    obs_level,
    obs_weight,
    innovation,
    obs_precision,
):
    level_count = control.shape[1]
    lat_cells = control.shape[2]
    lon_cells = control.shape[3]
    field_count = control.shape[0]
    flat_levels = field_count * level_count
    grid_gx = lax.axis_size("gx")
    grid_gy = lax.axis_size("gy")
    holders = grid_gx * grid_gy
    prof_count = prof_tile.shape[0]
    capacity = max(2, 2 * prof_count // holders)
    all_levels = level_count * lax.axis_size("obs")
    row_index = lax.axis_index("gy") * lat_cells + jnp.arange(lat_cells, dtype=jnp.int32)
    north_mask = (row_index != grid_gy * lat_cells - 1).astype(jnp.float32)
    east_own = diffusivity[0]
    north_own = diffusivity[1] * north_mask[None, :, None]
    west_column = passed_along(east_own[:, :, -1:], "gx", 1)
    south_row = shifted(north_own[:, -1:, :], "gy", 1)
    east_wide = jnp.concatenate([west_column, east_own, jnp.zeros_like(west_column)], axis=2)
    east_padded = jnp.pad(east_wide, ((0, 0), (1, 1), (0, 0)))
    north_tall = jnp.concatenate([south_row, north_own, jnp.zeros_like(south_row)], axis=1)
    north_padded = jnp.pad(north_tall, ((0, 0), (0, 0), (1, 1)))

    def diffuse(field):

        def sweep(step_index, values):
            rimmed = with_halo(values, (("gx", 3), ("gy", 2)), 1)
            return advance(rimmed, east_padded, north_padded)

        return lax.fori_loop(0, STEPS, sweep, field)

    increment = diffuse(control)
    flat_field = increment.reshape(flat_levels, lat_cells * lon_cells)
    holder_of = prof_tile[:, 0]
    one_hot = (holder_of[:, None] == jnp.arange(holders, dtype=jnp.int32)[None, :]).astype(
        jnp.int32
    )
    earlier = jnp.cumsum(one_hot, axis=0) - one_hot
    slot_of = jnp.sum(earlier * one_hot, axis=1)
    position = holder_of * capacity + slot_of
    requests = jnp.zeros((holders * capacity,), jnp.int32).at[position].set(prof_cell)
    asked = lax.all_to_all(
        requests.reshape(holders, 1, capacity),
        ("gx", "gy"),
        split_axis=0,
        concat_axis=0,
        tiled=True,
    )
    found = jnp.take(flat_field, asked[:, 0, :], axis=1)
    found = jnp.transpose(found, (1, 0, 2))
    returned = lax.all_to_all(found, ("gx", "gy"), split_axis=0, concat_axis=0, tiled=True)
    slab = jnp.transpose(returned, (1, 0, 2)).reshape(flat_levels, holders * capacity)[:, position]
    slab = slab.reshape(field_count, level_count, prof_count)
    columns = lax.all_gather(slab, "obs", axis=1, tiled=True)
    flat_columns = columns.reshape(-1)
    lower_index = (obs_field * all_levels + obs_level) * prof_count + obs_prof
    upper_index = lower_index + prof_count
    observed = (
        obs_weight * flat_columns[lower_index] + (1.0 - obs_weight) * flat_columns[upper_index]
    )
    departures = obs_precision * (observed - innovation)
    lower_share = obs_weight * departures
    upper_share = (1.0 - obs_weight) * departures
    targets = lax.all_gather(lower_index, "obs", axis=0, tiled=True)
    shares = lax.all_gather(jnp.stack([lower_share, upper_share]), "obs", axis=1, tiled=True)
    field_of = targets // (all_levels * prof_count)
    level_of = targets // prof_count % all_levels
    profile = targets % prof_count
    first_level = lax.axis_index("obs") * level_count

    def place(levels_hit, amounts):
        local_level = levels_hit - first_level
        inside = (local_level >= 0) & (local_level < level_count)
        index = (
            field_of * level_count + jnp.clip(local_level, 0, level_count - 1)
        ) * prof_count + profile
        return (index, jnp.where(inside, amounts, 0.0))

    index_low, amount_low = place(level_of, shares[0])
    index_high, amount_high = place(level_of + 1, shares[1])
    adjoint_slab = jnp.zeros((flat_levels * prof_count,), jnp.float32)
    adjoint_slab = adjoint_slab.at[index_low].add(amount_low).at[index_high].add(amount_high)
    adjoint_slab = adjoint_slab.reshape(flat_levels, prof_count)
    outgoing = (
        jnp.zeros((holders * capacity, flat_levels), jnp.float32).at[position].set(adjoint_slab.T)
    )
    outgoing = jnp.transpose(outgoing.reshape(holders, capacity, flat_levels), (0, 2, 1))
    incoming = lax.all_to_all(outgoing, ("gx", "gy"), split_axis=0, concat_axis=0, tiled=True)
    cells = asked.reshape(holders * capacity)
    amounts = jnp.transpose(incoming, (1, 0, 2)).reshape(flat_levels, holders * capacity)
    pulled = jnp.zeros((flat_levels, lat_cells * lon_cells), jnp.float32).at[:, cells].add(amounts)
    pulled = pulled.reshape(field_count, level_count, lat_cells, lon_cells)
    gradient = control + diffuse(pulled)
    return (gradient, departures)


def solution(mesh):
    in_specs = (
        P(None, "obs", "gy", "gx"),
        P(None, "obs", "gy", "gx"),
        P(("gx", "gy"), None),
        P(("gx", "gy")),
        P(("gx", "gy", "obs")),
        P(("gx", "gy", "obs")),
        P(("gx", "gy", "obs")),
        P(("gx", "gy", "obs")),
        P(("gx", "gy", "obs")),
        P(("gx", "gy", "obs")),
    )
    out_specs = (P(None, "obs", "gy", "gx"), P(("gx", "gy", "obs")))
    return jax.shard_map(
        per_device, mesh=mesh, in_specs=in_specs, out_specs=out_specs, check_vma=False
    )
```

profile of v0, /device:TPU:56, one launch (start us, length us, event | category | flops | bytes accessed | tf_op | source)
XLA Modules:
  0.0 557.8 jit_solution(11405129827567170340)
XLA Ops:
  7.6 9.9 %all-to-all-start = ((s32[64,1,16]{2,1,0:T(1,128)}), s32[64,1,16]{2,1,0:T(1,128)S(1)}, u32[]{:S(2)}, u32[]{:S(2)}) async-start(s32[64,1,16]{2,1,0:T(1,128)} %bitcast.13), calls=%async_computation | async-start | bytes 65536 | tf_op jit(solution)/shard_map/all_to_all | solution.py:95
  21.5 27.4 %all-gather.1 = s32[8,1,512]{2,1,0:T(1,128)S(1)} all-gather(s32[1,1,512]{2,1,0:T(1,128)S(1)} %bitcast.97), channel_id=1, replica_groups=mesh['gx'=8,'gy'=8,'obs'=8] {'obs'}, dimensions={0}, use_global_device_ids=true | all-gather | bytes 18432 | tf_op jit(solution)/shard_map/all_gather | solution.py:117
  50.4 168.9 %while.20 = (s32[]{:T(128)}, f32[4,1,128,128]{3,2,1,0:T(8,128)S(1)}, f32[1,130,130]{2,1,0:T(8,128)S(1)}, f32[1,130,130]{2,1,0:T(8,128)S(1)}, s32[]{:T(128)}) while((s32[]{:T(128)}, f32[4,1,128,128]{3,2,1,0:T(8,128)S(1)}, f32[1,130,130]{2,1,0:T(8,128)S(1)}, f32[1,130,130]{2,1,0:T(8,128)S(1)}, s32[]{:T(128)}) %tuple.68), condition=%wide.region_5.6_spmd, body=%wide.region_4.5_spmd.sunk | while | flops 1312802 | bytes 2155101 | solution.py:83
  51.1 3.4 collective-permute-done
  54.4 3.2 collective-permute-done.1
  57.8 4.3 collective-permute-start.2
  64.3 4.6 collective-permute-done.3
  70.0 3.4 collective-permute-done
  73.4 3.1 collective-permute-done.1
  78.8 3.7 collective-permute-start.3
  86.6 3.4 collective-permute-done
  90.0 3.1 collective-permute-done.1
  99.2 3.6 collective-permute-done.3
  103.9 3.4 collective-permute-done
  116.5 3.4 collective-permute-done.3
  121.1 3.4 collective-permute-done
  130.2 3.4 collective-permute-start.3
  133.7 3.2 collective-permute-done.3
  138.0 3.4 collective-permute-done
  146.6 3.9 collective-permute-start.3
  154.4 3.4 collective-permute-done
  162.9 3.9 collective-permute-start.3
  170.8 3.4 collective-permute-done
  179.3 3.9 collective-permute-start.3
  187.2 3.4 collective-permute-done
  195.7 3.9 collective-permute-start.3
  203.5 3.4 collective-permute-done
  212.1 3.9 collective-permute-start.3
  219.3 4.7 copy.30
  224.0 6.2 %gather_fusion = f32[1024,4]{1,0:T(8,128)S(1)} fusion(f32[4,16384]{0,1:T(8,128)} %bitcast.79, s32[1024]{0:T(1024)S(1)} %broadcast_clamp_fusion), kind=kCustom, calls=%fused_computation | custom fusion | bytes 36864 | tf_op jit(solution)/shard_map/jit(_take)/gather | solution.py:102
  231.4 6.3 %all-to-all-start.1 = ((f32[64,4,16]{2,1,0:T(4,128)}), f32[64,4,16]{2,1,0:T(4,128)S(1)}, u32[]{:S(2)}, u32[]{:S(2)}) async-start(f32[64,4,16]{2,1,0:T(4,128)} %select_bitcast_fusion), calls=%async_computation.1 | async-start | bytes 262144 | tf_op jit(solution)/shard_map/all_to_all | solution.py:104
  239.1 7.9 %all-to-all-done.1 = f32[64,4,16]{2,1,0:T(4,128)S(1)} async-done(((f32[64,4,16]{2,1,0:T(4,128)}), f32[64,4,16]{2,1,0:T(4,128)S(1)}, u32[]{:S(2)}, u32[]{:S(2)}) %all-to-all-start.1) | async-done | bytes 16416 | tf_op jit(solution)/shard_map/all_to_all | solution.py:104
  248.5 29.7 %all-gather = f32[4,4096]{0,1:T(8,128)S(1)} all-gather(f32[4,512]{0,1:T(8,128)S(1)} %bitcast.87), channel_id=2, replica_groups=mesh['gx'=8,'gy'=8,'obs'=8] {'obs'}, dimensions={1}, use_global_device_ids=true | all-gather | bytes 73728 | tf_op jit(solution)/shard_map/all_gather | solution.py:107
  278.9 3.1 gather_fusion.3
  282.0 3.1 gather_fusion.2
  285.3 24.7 %all_gather.11 = f32[2,4096]{1,0:T(2,128)S(1)} all-gather(f32[2,512]{1,0:T(2,128)S(1)} %pad_maximum_fusion.22), channel_id=1, replica_groups=mesh['gx'=8,'gy'=8,'obs'=8] {'obs'}, dimensions={1}, use_global_device_ids=true | all-gather | bytes 36864 | tf_op jit(solution)/shard_map/all_gather | solution.py:118
  310.0 22.2 %scatter_custom_fusion.1 = f32[2048]{0:T(1024)S(1)} fusion(s32[4096]{0:T(1024)S(1)} %get-tuple-element.109, f32[4096]{0:T(1024)S(1)} %get-tuple-element.107, f32[]{:T(128)} %constant.94.clone.1), kind=kCustom, calls=%fused_computation.113 | custom fusion | flops 4096 | bytes 8196 | tf_op jit(solution)/shard_map/scatter-add | solution.py:135
  332.2 22.8 %scatter_fusion = f32[2048]{0:T(1024)S(1)} fusion(f32[2048]{0:T(1024)S(1)} %scatter_custom_fusion.1, s32[4096]{0:T(1024)S(1)} %get-tuple-element.108, f32[4096]{0:T(1024)S(1)} %get-tuple-element.106), kind=kCustom, calls=%fused_computation.6 | custom fusion | flops 4096 | bytes 65536 | tf_op jit(solution)/shard_map/scatter-add | solution.py:135
  358.0 6.2 %all-to-all-start.2 = ((f32[64,4,16]{2,1,0:T(4,128)}), f32[64,4,16]{2,1,0:T(4,128)S(1)}, u32[]{:S(2)}, u32[]{:S(2)}) async-start(f32[64,4,16]{2,1,0:T(4,128)} %bitcast.33), calls=%async_computation.2 | async-start | bytes 262144 | tf_op jit(solution)/shard_map/all_to_all | solution.py:141
  364.2 9.2 %all-to-all-done.2 = f32[64,4,16]{2,1,0:T(4,128)S(1)} async-done(((f32[64,4,16]{2,1,0:T(4,128)}), f32[64,4,16]{2,1,0:T(4,128)S(1)}, u32[]{:S(2)}, u32[]{:S(2)}) %all-to-all-start.2) | async-done | bytes 16416 | tf_op jit(solution)/shard_map/all_to_all | solution.py:141
  373.8 9.9 %scatter_custom_fusion.4 = f32[4,16384]{0,1:T(8,128)} fusion(s32[1024]{0:T(1024)S(1)} %bitcast.104, f32[1024,4]{1,0:T(8,128)S(1)} %copy.37, f32[]{:T(128)} %constant.94.clone.1), kind=kCustom, calls=%fused_computation.63 | custom fusion | flops 4096 | bytes 262148 | tf_op jit(solution)/shard_map/scatter-add | solution.py:144
  383.7 5.2 copy.38
  388.9 168.2 %while.21 = (s32[]{:T(128)}, f32[4,1,128,128]{3,2,1,0:T(8,128)S(1)}, f32[1,130,130]{2,1,0:T(8,128)S(1)}, f32[1,130,130]{2,1,0:T(8,128)S(1)}, s32[]{:T(128)}) while((s32[]{:T(128)}, f32[4,1,128,128]{3,2,1,0:T(8,128)S(1)}, f32[1,130,130]{2,1,0:T(8,128)S(1)}, f32[1,130,130]{2,1,0:T(8,128)S(1)}, s32[]{:T(128)}) %tuple.75), condition=%wide.region_11.12_spmd, body=%wide.region_10.11_spmd.sunk | while | flops 1312802 | bytes 2155101 | solution.py:83
  389.6 3.6 collective-permute-done.4
  396.5 4.1 collective-permute-start.6
  402.6 4.6 collective-permute-done.7
  408.4 3.4 collective-permute-done.4
  416.9 3.9 collective-permute-start.7
  424.8 3.4 collective-permute-done.4
  433.3 3.9 collective-permute-start.7
  441.2 3.4 collective-permute-done.4
  449.7 3.9 collective-permute-start.7
  457.5 3.4 collective-permute-done.4
  466.1 3.9 collective-permute-start.7
  473.9 3.4 collective-permute-done.4
  482.5 3.9 collective-permute-start.7
  490.3 3.4 collective-permute-done.4
  499.2 3.5 collective-permute-start.7
  507.1 3.4 collective-permute-done.4
  519.7 3.4 collective-permute-done.7
  524.2 3.4 collective-permute-done.4
  536.8 3.4 collective-permute-done.7
  541.4 3.4 collective-permute-done.4
  550.0 3.9 collective-permute-start.7
  (282 shorter events, 190.7 us)
Async XLA Ops:
  7.6 216.3 %all-to-all-start = ((s32[64,1,16]{2,1,0:T(1,128)}), s32[64,1,16]{2,1,0:T(1,128)S(1)}, u32[]{:S(2)}, u32[]{:S(2)}) async-start(s32[64,1,16]{2,1,0:T(1,128)} %bitcast.13), calls=%async_computation | async-start | bytes 65536 | tf_op jit(solution)/shard_map/all_to_all | solution.py:95
  18.5 31.6 %collective-permute-start.9 = (f32[1,1,128]{2,1,0:T(1,128)S(1)}, f32[1,1,128]{2,1,0:T(1,128)S(1)}, u32[]{:S(2)}, u32[]{:S(2)}) collective-permute-start(f32[1,1,128]{2,1,0:T(1,128)S(1)} %slice.122), channel_id=1, source_target_pairs={{0,8},{8,16},{16,24},{24,32},{32,40},{40,48},{48,56},{1,9},{9,17},... | collective-permute-start | bytes 1544 | tf_op jit(solution)/shard_map/ppermute | solution.py:17
  20.7 29.5 %collective-permute-start.8 = (f32[1,128,1]{2,1,0:T(8,128)S(1)}, f32[1,128,1]{2,1,0:T(8,128)S(1)}, u32[]{:S(2)}, u32[]{:S(2)}) collective-permute-start(f32[1,128,1]{2,1,0:T(8,128)S(1)} %slice.121), channel_id=1, source_target_pairs={{0,64},{64,128},{128,192},{192,256},{256,320},{320,384},{384,448},... | collective-permute-start | bytes 1544 | tf_op jit(solution)/shard_map/ppermute | solution.py:11
  50.6 7.1 %collective-permute-start.1 = (f32[4,1,128,1]{3,2,1,0:T(8,128)S(1)}, f32[4,1,128,1]{3,2,1,0:T(8,128)S(1)}, u32[]{:S(2)}, u32[]{:S(2)}) collective-permute-start(f32[4,1,128,1]{3,2,1,0:T(8,128)S(1)} %get-tuple-element.173), channel_id=1, source_target_pairs={{0,64},{64,128},{128,192},{192,256},{256,320},{320,384},{384,448},... | collective-permute-start | bytes 6152 | tf_op jit(solution)/shard_map/while/body/eval_jaxpr/ppermute | solution.py:26
  57.8 6.5 %collective-permute-start.2 = (f32[4,1,1,130]{3,2,1,0:T(1,128)S(1)}, f32[4,1,1,130]{3,2,1,0:T(1,128)S(1)}, u32[]{:S(2)}, u32[]{:S(2)}) collective-permute-start(f32[4,1,1,130]{3,2,1,0:T(1,128)S(1)} %get-tuple-element.174), channel_id=1, source_target_pairs={{0,8},{8,16},{16,24},{24,32},{32,40},{40,48},{48,56},{56,0},{1,9},... | collective-permute-start | bytes 6248 | tf_op jit(solution)/shard_map/while/body/eval_jaxpr/ppermute | solution.py:26
  62.1 6.7 %collective-permute-start.3 = (f32[4,1,1,130]{3,2,1,0:T(1,128)S(1)}, f32[4,1,1,130]{3,2,1,0:T(1,128)S(1)}, u32[]{:S(2)}, u32[]{:S(2)}) collective-permute-start(f32[4,1,1,130]{3,2,1,0:T(1,128)S(1)} %get-tuple-element.175), channel_id=1, source_target_pairs={{8,0},{16,8},{24,16},{32,24},{40,32},{48,40},{56,48},{0,56},{9,1},... | collective-permute-start | bytes 6248 | tf_op jit(solution)/shard_map/while/body/eval_jaxpr/ppermute | solution.py:29
  69.5 7.0 %collective-permute-start.1 = (f32[4,1,128,1]{3,2,1,0:T(8,128)S(1)}, f32[4,1,128,1]{3,2,1,0:T(8,128)S(1)}, u32[]{:S(2)}, u32[]{:S(2)}) collective-permute-start(f32[4,1,128,1]{3,2,1,0:T(8,128)S(1)} %get-tuple-element.173), channel_id=1, source_target_pairs={{0,64},{64,128},{128,192},{192,256},{256,320},{320,384},{384,448},... | collective-permute-start | bytes 6152 | tf_op jit(solution)/shard_map/while/body/eval_jaxpr/ppermute | solution.py:26
  76.6 6.0 %collective-permute-start.2 = (f32[4,1,1,130]{3,2,1,0:T(1,128)S(1)}, f32[4,1,1,130]{3,2,1,0:T(1,128)S(1)}, u32[]{:S(2)}, u32[]{:S(2)}) collective-permute-start(f32[4,1,1,130]{3,2,1,0:T(1,128)S(1)} %get-tuple-element.174), channel_id=1, source_target_pairs={{0,8},{8,16},{16,24},{24,32},{32,40},{40,48},{48,56},{56,0},{1,9},... | collective-permute-start | bytes 6248 | tf_op jit(solution)/shard_map/while/body/eval_jaxpr/ppermute | solution.py:26
  78.8 6.7 %collective-permute-start.3 = (f32[4,1,1,130]{3,2,1,0:T(1,128)S(1)}, f32[4,1,1,130]{3,2,1,0:T(1,128)S(1)}, u32[]{:S(2)}, u32[]{:S(2)}) collective-permute-start(f32[4,1,1,130]{3,2,1,0:T(1,128)S(1)} %get-tuple-element.175), channel_id=1, source_target_pairs={{8,0},{16,8},{24,16},{32,24},{40,32},{48,40},{56,48},{0,56},{9,1},... | collective-permute-start | bytes 6248 | tf_op jit(solution)/shard_map/while/body/eval_jaxpr/ppermute | solution.py:29
  86.1 7.0 %collective-permute-start.1 = (f32[4,1,128,1]{3,2,1,0:T(8,128)S(1)}, f32[4,1,128,1]{3,2,1,0:T(8,128)S(1)}, u32[]{:S(2)}, u32[]{:S(2)}) collective-permute-start(f32[4,1,128,1]{3,2,1,0:T(8,128)S(1)} %get-tuple-element.173), channel_id=1, source_target_pairs={{0,64},{64,128},{128,192},{192,256},{256,320},{320,384},{384,448},... | collective-permute-start | bytes 6152 | tf_op jit(solution)/shard_map/while/body/eval_jaxpr/ppermute | solution.py:26
  93.2 6.0 %collective-permute-start.2 = (f32[4,1,1,130]{3,2,1,0:T(1,128)S(1)}, f32[4,1,1,130]{3,2,1,0:T(1,128)S(1)}, u32[]{:S(2)}, u32[]{:S(2)}) collective-permute-start(f32[4,1,1,130]{3,2,1,0:T(1,128)S(1)} %get-tuple-element.174), channel_id=1, source_target_pairs={{0,8},{8,16},{16,24},{24,32},{32,40},{40,48},{48,56},{56,0},{1,9},... | collective-permute-start | bytes 6248 | tf_op jit(solution)/shard_map/while/body/eval_jaxpr/ppermute | solution.py:26
  96.1 6.7 %collective-permute-start.3 = (f32[4,1,1,130]{3,2,1,0:T(1,128)S(1)}, f32[4,1,1,130]{3,2,1,0:T(1,128)S(1)}, u32[]{:S(2)}, u32[]{:S(2)}) collective-permute-start(f32[4,1,1,130]{3,2,1,0:T(1,128)S(1)} %get-tuple-element.175), channel_id=1, source_target_pairs={{8,0},{16,8},{24,16},{32,24},{40,32},{48,40},{56,48},{0,56},{9,1},... | collective-permute-start | bytes 6248 | tf_op jit(solution)/shard_map/while/body/eval_jaxpr/ppermute | solution.py:29
  103.4 7.0 %collective-permute-start.1 = (f32[4,1,128,1]{3,2,1,0:T(8,128)S(1)}, f32[4,1,128,1]{3,2,1,0:T(8,128)S(1)}, u32[]{:S(2)}, u32[]{:S(2)}) collective-permute-start(f32[4,1,128,1]{3,2,1,0:T(8,128)S(1)} %get-tuple-element.173), channel_id=1, source_target_pairs={{0,64},{64,128},{128,192},{192,256},{256,320},{320,384},{384,448},... | collective-permute-start | bytes 6152 | tf_op jit(solution)/shard_map/while/body/eval_jaxpr/ppermute | solution.py:26
  110.5 6.0 %collective-permute-start.2 = (f32[4,1,1,130]{3,2,1,0:T(1,128)S(1)}, f32[4,1,1,130]{3,2,1,0:T(1,128)S(1)}, u32[]{:S(2)}, u32[]{:S(2)}) collective-permute-start(f32[4,1,1,130]{3,2,1,0:T(1,128)S(1)} %get-tuple-element.174), channel_id=1, source_target_pairs={{0,8},{8,16},{16,24},{24,32},{32,40},{40,48},{48,56},{56,0},{1,9},... | collective-permute-start | bytes 6248 | tf_op jit(solution)/shard_map/while/body/eval_jaxpr/ppermute | solution.py:26
  113.2 6.7 %collective-permute-start.3 = (f32[4,1,1,130]{3,2,1,0:T(1,128)S(1)}, f32[4,1,1,130]{3,2,1,0:T(1,128)S(1)}, u32[]{:S(2)}, u32[]{:S(2)}) collective-permute-start(f32[4,1,1,130]{3,2,1,0:T(1,128)S(1)} %get-tuple-element.175), channel_id=1, source_target_pairs={{8,0},{16,8},{24,16},{32,24},{40,32},{48,40},{56,48},{0,56},{9,1},... | collective-permute-start | bytes 6248 | tf_op jit(solution)/shard_map/while/body/eval_jaxpr/ppermute | solution.py:29
  120.6 7.0 %collective-permute-start.1 = (f32[4,1,128,1]{3,2,1,0:T(8,128)S(1)}, f32[4,1,128,1]{3,2,1,0:T(8,128)S(1)}, u32[]{:S(2)}, u32[]{:S(2)}) collective-permute-start(f32[4,1,128,1]{3,2,1,0:T(8,128)S(1)} %get-tuple-element.173), channel_id=1, source_target_pairs={{0,64},{64,128},{128,192},{192,256},{256,320},{320,384},{384,448},... | collective-permute-start | bytes 6152 | tf_op jit(solution)/shard_map/while/body/eval_jaxpr/ppermute | solution.py:26
  127.7 6.0 %collective-permute-start.2 = (f32[4,1,1,130]{3,2,1,0:T(1,128)S(1)}, f32[4,1,1,130]{3,2,1,0:T(1,128)S(1)}, u32[]{:S(2)}, u32[]{:S(2)}) collective-permute-start(f32[4,1,1,130]{3,2,1,0:T(1,128)S(1)} %get-tuple-element.174), channel_id=1, source_target_pairs={{0,8},{8,16},{16,24},{24,32},{32,40},{40,48},{48,56},{56,0},{1,9},... | collective-permute-start | bytes 6248 | tf_op jit(solution)/shard_map/while/body/eval_jaxpr/ppermute | solution.py:26
  130.2 6.7 %collective-permute-start.3 = (f32[4,1,1,130]{3,2,1,0:T(1,128)S(1)}, f32[4,1,1,130]{3,2,1,0:T(1,128)S(1)}, u32[]{:S(2)}, u32[]{:S(2)}) collective-permute-start(f32[4,1,1,130]{3,2,1,0:T(1,128)S(1)} %get-tuple-element.175), channel_id=1, source_target_pairs={{8,0},{16,8},{24,16},{32,24},{40,32},{48,40},{56,48},{0,56},{9,1},... | collective-permute-start | bytes 6248 | tf_op jit(solution)/shard_map/while/body/eval_jaxpr/ppermute | solution.py:29
  137.5 7.0 %collective-permute-start.1 = (f32[4,1,128,1]{3,2,1,0:T(8,128)S(1)}, f32[4,1,128,1]{3,2,1,0:T(8,128)S(1)}, u32[]{:S(2)}, u32[]{:S(2)}) collective-permute-start(f32[4,1,128,1]{3,2,1,0:T(8,128)S(1)} %get-tuple-element.173), channel_id=1, source_target_pairs={{0,64},{64,128},{128,192},{192,256},{256,320},{320,384},{384,448},... | collective-permute-start | bytes 6152 | tf_op jit(solution)/shard_map/while/body/eval_jaxpr/ppermute | solution.py:26
  144.6 6.0 %collective-permute-start.2 = (f32[4,1,1,130]{3,2,1,0:T(1,128)S(1)}, f32[4,1,1,130]{3,2,1,0:T(1,128)S(1)}, u32[]{:S(2)}, u32[]{:S(2)}) collective-permute-start(f32[4,1,1,130]{3,2,1,0:T(1,128)S(1)} %get-tuple-element.174), channel_id=1, source_target_pairs={{0,8},{8,16},{16,24},{24,32},{32,40},{40,48},{48,56},{56,0},{1,9},... | collective-permute-start | bytes 6248 | tf_op jit(solution)/shard_map/while/body/eval_jaxpr/ppermute | solution.py:26
  146.6 6.7 %collective-permute-start.3 = (f32[4,1,1,130]{3,2,1,0:T(1,128)S(1)}, f32[4,1,1,130]{3,2,1,0:T(1,128)S(1)}, u32[]{:S(2)}, u32[]{:S(2)}) collective-permute-start(f32[4,1,1,130]{3,2,1,0:T(1,128)S(1)} %get-tuple-element.175), channel_id=1, source_target_pairs={{8,0},{16,8},{24,16},{32,24},{40,32},{48,40},{56,48},{0,56},{9,1},... | collective-permute-start | bytes 6248 | tf_op jit(solution)/shard_map/while/body/eval_jaxpr/ppermute | solution.py:29
  153.9 7.0 %collective-permute-start.1 = (f32[4,1,128,1]{3,2,1,0:T(8,128)S(1)}, f32[4,1,128,1]{3,2,1,0:T(8,128)S(1)}, u32[]{:S(2)}, u32[]{:S(2)}) collective-permute-start(f32[4,1,128,1]{3,2,1,0:T(8,128)S(1)} %get-tuple-element.173), channel_id=1, source_target_pairs={{0,64},{64,128},{128,192},{192,256},{256,320},{320,384},{384,448},... | collective-permute-start | bytes 6152 | tf_op jit(solution)/shard_map/while/body/eval_jaxpr/ppermute | solution.py:26
  161.0 6.0 %collective-permute-start.2 = (f32[4,1,1,130]{3,2,1,0:T(1,128)S(1)}, f32[4,1,1,130]{3,2,1,0:T(1,128)S(1)}, u32[]{:S(2)}, u32[]{:S(2)}) collective-permute-start(f32[4,1,1,130]{3,2,1,0:T(1,128)S(1)} %get-tuple-element.174), channel_id=1, source_target_pairs={{0,8},{8,16},{16,24},{24,32},{32,40},{40,48},{48,56},{56,0},{1,9},... | collective-permute-start | bytes 6248 | tf_op jit(solution)/shard_map/while/body/eval_jaxpr/ppermute | solution.py:26
  162.9 6.7 %collective-permute-start.3 = (f32[4,1,1,130]{3,2,1,0:T(1,128)S(1)}, f32[4,1,1,130]{3,2,1,0:T(1,128)S(1)}, u32[]{:S(2)}, u32[]{:S(2)}) collective-permute-start(f32[4,1,1,130]{3,2,1,0:T(1,128)S(1)} %get-tuple-element.175), channel_id=1, source_target_pairs={{8,0},{16,8},{24,16},{32,24},{40,32},{48,40},{56,48},{0,56},{9,1},... | collective-permute-start | bytes 6248 | tf_op jit(solution)/shard_map/while/body/eval_jaxpr/ppermute | solution.py:29
  170.3 7.0 %collective-permute-start.1 = (f32[4,1,128,1]{3,2,1,0:T(8,128)S(1)}, f32[4,1,128,1]{3,2,1,0:T(8,128)S(1)}, u32[]{:S(2)}, u32[]{:S(2)}) collective-permute-start(f32[4,1,128,1]{3,2,1,0:T(8,128)S(1)} %get-tuple-element.173), channel_id=1, source_target_pairs={{0,64},{64,128},{128,192},{192,256},{256,320},{320,384},{384,448},... | collective-permute-start | bytes 6152 | tf_op jit(solution)/shard_map/while/body/eval_jaxpr/ppermute | solution.py:26
  177.4 6.0 %collective-permute-start.2 = (f32[4,1,1,130]{3,2,1,0:T(1,128)S(1)}, f32[4,1,1,130]{3,2,1,0:T(1,128)S(1)}, u32[]{:S(2)}, u32[]{:S(2)}) collective-permute-start(f32[4,1,1,130]{3,2,1,0:T(1,128)S(1)} %get-tuple-element.174), channel_id=1, source_target_pairs={{0,8},{8,16},{16,24},{24,32},{32,40},{40,48},{48,56},{56,0},{1,9},... | collective-permute-start | bytes 6248 | tf_op jit(solution)/shard_map/while/body/eval_jaxpr/ppermute | solution.py:26
  179.3 6.7 %collective-permute-start.3 = (f32[4,1,1,130]{3,2,1,0:T(1,128)S(1)}, f32[4,1,1,130]{3,2,1,0:T(1,128)S(1)}, u32[]{:S(2)}, u32[]{:S(2)}) collective-permute-start(f32[4,1,1,130]{3,2,1,0:T(1,128)S(1)} %get-tuple-element.175), channel_id=1, source_target_pairs={{8,0},{16,8},{24,16},{32,24},{40,32},{48,40},{56,48},{0,56},{9,1},... | collective-permute-start | bytes 6248 | tf_op jit(solution)/shard_map/while/body/eval_jaxpr/ppermute | solution.py:29
  186.7 7.0 %collective-permute-start.1 = (f32[4,1,128,1]{3,2,1,0:T(8,128)S(1)}, f32[4,1,128,1]{3,2,1,0:T(8,128)S(1)}, u32[]{:S(2)}, u32[]{:S(2)}) collective-permute-start(f32[4,1,128,1]{3,2,1,0:T(8,128)S(1)} %get-tuple-element.173), channel_id=1, source_target_pairs={{0,64},{64,128},{128,192},{192,256},{256,320},{320,384},{384,448},... | collective-permute-start | bytes 6152 | tf_op jit(solution)/shard_map/while/body/eval_jaxpr/ppermute | solution.py:26
  193.8 6.0 %collective-permute-start.2 = (f32[4,1,1,130]{3,2,1,0:T(1,128)S(1)}, f32[4,1,1,130]{3,2,1,0:T(1,128)S(1)}, u32[]{:S(2)}, u32[]{:S(2)}) collective-permute-start(f32[4,1,1,130]{3,2,1,0:T(1,128)S(1)} %get-tuple-element.174), channel_id=1, source_target_pairs={{0,8},{8,16},{16,24},{24,32},{32,40},{40,48},{48,56},{56,0},{1,9},... | collective-permute-start | bytes 6248 | tf_op jit(solution)/shard_map/while/body/eval_jaxpr/ppermute | solution.py:26
  195.7 6.7 %collective-permute-start.3 = (f32[4,1,1,130]{3,2,1,0:T(1,128)S(1)}, f32[4,1,1,130]{3,2,1,0:T(1,128)S(1)}, u32[]{:S(2)}, u32[]{:S(2)}) collective-permute-start(f32[4,1,1,130]{3,2,1,0:T(1,128)S(1)} %get-tuple-element.175), channel_id=1, source_target_pairs={{8,0},{16,8},{24,16},{32,24},{40,32},{48,40},{56,48},{0,56},{9,1},... | collective-permute-start | bytes 6248 | tf_op jit(solution)/shard_map/while/body/eval_jaxpr/ppermute | solution.py:29
  203.0 7.0 %collective-permute-start.1 = (f32[4,1,128,1]{3,2,1,0:T(8,128)S(1)}, f32[4,1,128,1]{3,2,1,0:T(8,128)S(1)}, u32[]{:S(2)}, u32[]{:S(2)}) collective-permute-start(f32[4,1,128,1]{3,2,1,0:T(8,128)S(1)} %get-tuple-element.173), channel_id=1, source_target_pairs={{0,64},{64,128},{128,192},{192,256},{256,320},{320,384},{384,448},... | collective-permute-start | bytes 6152 | tf_op jit(solution)/shard_map/while/body/eval_jaxpr/ppermute | solution.py:26
  210.2 6.0 %collective-permute-start.2 = (f32[4,1,1,130]{3,2,1,0:T(1,128)S(1)}, f32[4,1,1,130]{3,2,1,0:T(1,128)S(1)}, u32[]{:S(2)}, u32[]{:S(2)}) collective-permute-start(f32[4,1,1,130]{3,2,1,0:T(1,128)S(1)} %get-tuple-element.174), channel_id=1, source_target_pairs={{0,8},{8,16},{16,24},{24,32},{32,40},{40,48},{48,56},{56,0},{1,9},... | collective-permute-start | bytes 6248 | tf_op jit(solution)/shard_map/while/body/eval_jaxpr/ppermute | solution.py:26
  212.1 6.7 %collective-permute-start.3 = (f32[4,1,1,130]{3,2,1,0:T(1,128)S(1)}, f32[4,1,1,130]{3,2,1,0:T(1,128)S(1)}, u32[]{:S(2)}, u32[]{:S(2)}) collective-permute-start(f32[4,1,1,130]{3,2,1,0:T(1,128)S(1)} %get-tuple-element.175), channel_id=1, source_target_pairs={{8,0},{16,8},{24,16},{32,24},{40,32},{48,40},{56,48},{0,56},{9,1},... | collective-permute-start | bytes 6248 | tf_op jit(solution)/shard_map/while/body/eval_jaxpr/ppermute | solution.py:29
  231.4 15.6 %all-to-all-start.1 = ((f32[64,4,16]{2,1,0:T(4,128)}), f32[64,4,16]{2,1,0:T(4,128)S(1)}, u32[]{:S(2)}, u32[]{:S(2)}) async-start(f32[64,4,16]{2,1,0:T(4,128)} %select_bitcast_fusion), calls=%async_computation.1 | async-start | bytes 262144 | tf_op jit(solution)/shard_map/all_to_all | solution.py:104
  358.0 15.4 %all-to-all-start.2 = ((f32[64,4,16]{2,1,0:T(4,128)}), f32[64,4,16]{2,1,0:T(4,128)S(1)}, u32[]{:S(2)}, u32[]{:S(2)}) async-start(f32[64,4,16]{2,1,0:T(4,128)} %bitcast.33), calls=%async_computation.2 | async-start | bytes 262144 | tf_op jit(solution)/shard_map/all_to_all | solution.py:141
  389.4 7.0 %collective-permute-start.5 = (f32[4,1,128,1]{3,2,1,0:T(8,128)S(1)}, f32[4,1,128,1]{3,2,1,0:T(8,128)S(1)}, u32[]{:S(2)}, u32[]{:S(2)}) collective-permute-start(f32[4,1,128,1]{3,2,1,0:T(8,128)S(1)} %get-tuple-element.185), channel_id=1, source_target_pairs={{0,64},{64,128},{128,192},{192,256},{256,320},{320,384},{384,448},... | collective-permute-start | bytes 6152 | tf_op jit(solution)/shard_map/while/body/eval_jaxpr/ppermute | solution.py:26
  396.5 6.1 %collective-permute-start.6 = (f32[4,1,1,130]{3,2,1,0:T(1,128)S(1)}, f32[4,1,1,130]{3,2,1,0:T(1,128)S(1)}, u32[]{:S(2)}, u32[]{:S(2)}) collective-permute-start(f32[4,1,1,130]{3,2,1,0:T(1,128)S(1)} %get-tuple-element.186), channel_id=1, source_target_pairs={{0,8},{8,16},{16,24},{24,32},{32,40},{40,48},{48,56},{56,0},{1,9},... | collective-permute-start | bytes 6248 | tf_op jit(solution)/shard_map/while/body/eval_jaxpr/ppermute | solution.py:26
  400.6 6.7 %collective-permute-start.7 = (f32[4,1,1,130]{3,2,1,0:T(1,128)S(1)}, f32[4,1,1,130]{3,2,1,0:T(1,128)S(1)}, u32[]{:S(2)}, u32[]{:S(2)}) collective-permute-start(f32[4,1,1,130]{3,2,1,0:T(1,128)S(1)} %get-tuple-element.187), channel_id=1, source_target_pairs={{8,0},{16,8},{24,16},{32,24},{40,32},{48,40},{56,48},{0,56},{9,1},... | collective-permute-start | bytes 6248 | tf_op jit(solution)/shard_map/while/body/eval_jaxpr/ppermute | solution.py:29
  407.9 7.0 %collective-permute-start.5 = (f32[4,1,128,1]{3,2,1,0:T(8,128)S(1)}, f32[4,1,128,1]{3,2,1,0:T(8,128)S(1)}, u32[]{:S(2)}, u32[]{:S(2)}) collective-permute-start(f32[4,1,128,1]{3,2,1,0:T(8,128)S(1)} %get-tuple-element.185), channel_id=1, source_target_pairs={{0,64},{64,128},{128,192},{192,256},{256,320},{320,384},{384,448},... | collective-permute-start | bytes 6152 | tf_op jit(solution)/shard_map/while/body/eval_jaxpr/ppermute | solution.py:26
  415.0 6.0 %collective-permute-start.6 = (f32[4,1,1,130]{3,2,1,0:T(1,128)S(1)}, f32[4,1,1,130]{3,2,1,0:T(1,128)S(1)}, u32[]{:S(2)}, u32[]{:S(2)}) collective-permute-start(f32[4,1,1,130]{3,2,1,0:T(1,128)S(1)} %get-tuple-element.186), channel_id=1, source_target_pairs={{0,8},{8,16},{16,24},{24,32},{32,40},{40,48},{48,56},{56,0},{1,9},... | collective-permute-start | bytes 6248 | tf_op jit(solution)/shard_map/while/body/eval_jaxpr/ppermute | solution.py:26
  416.9 6.7 %collective-permute-start.7 = (f32[4,1,1,130]{3,2,1,0:T(1,128)S(1)}, f32[4,1,1,130]{3,2,1,0:T(1,128)S(1)}, u32[]{:S(2)}, u32[]{:S(2)}) collective-permute-start(f32[4,1,1,130]{3,2,1,0:T(1,128)S(1)} %get-tuple-element.187), channel_id=1, source_target_pairs={{8,0},{16,8},{24,16},{32,24},{40,32},{48,40},{56,48},{0,56},{9,1},... | collective-permute-start | bytes 6248 | tf_op jit(solution)/shard_map/while/body/eval_jaxpr/ppermute | solution.py:29
  424.3 7.0 %collective-permute-start.5 = (f32[4,1,128,1]{3,2,1,0:T(8,128)S(1)}, f32[4,1,128,1]{3,2,1,0:T(8,128)S(1)}, u32[]{:S(2)}, u32[]{:S(2)}) collective-permute-start(f32[4,1,128,1]{3,2,1,0:T(8,128)S(1)} %get-tuple-element.185), channel_id=1, source_target_pairs={{0,64},{64,128},{128,192},{192,256},{256,320},{320,384},{384,448},... | collective-permute-start | bytes 6152 | tf_op jit(solution)/shard_map/while/body/eval_jaxpr/ppermute | solution.py:26
  431.4 6.0 %collective-permute-start.6 = (f32[4,1,1,130]{3,2,1,0:T(1,128)S(1)}, f32[4,1,1,130]{3,2,1,0:T(1,128)S(1)}, u32[]{:S(2)}, u32[]{:S(2)}) collective-permute-start(f32[4,1,1,130]{3,2,1,0:T(1,128)S(1)} %get-tuple-element.186), channel_id=1, source_target_pairs={{0,8},{8,16},{16,24},{24,32},{32,40},{40,48},{48,56},{56,0},{1,9},... | collective-permute-start | bytes 6248 | tf_op jit(solution)/shard_map/while/body/eval_jaxpr/ppermute | solution.py:26
  433.3 6.7 %collective-permute-start.7 = (f32[4,1,1,130]{3,2,1,0:T(1,128)S(1)}, f32[4,1,1,130]{3,2,1,0:T(1,128)S(1)}, u32[]{:S(2)}, u32[]{:S(2)}) collective-permute-start(f32[4,1,1,130]{3,2,1,0:T(1,128)S(1)} %get-tuple-element.187), channel_id=1, source_target_pairs={{8,0},{16,8},{24,16},{32,24},{40,32},{48,40},{56,48},{0,56},{9,1},... | collective-permute-start | bytes 6248 | tf_op jit(solution)/shard_map/while/body/eval_jaxpr/ppermute | solution.py:29
  440.7 7.0 %collective-permute-start.5 = (f32[4,1,128,1]{3,2,1,0:T(8,128)S(1)}, f32[4,1,128,1]{3,2,1,0:T(8,128)S(1)}, u32[]{:S(2)}, u32[]{:S(2)}) collective-permute-start(f32[4,1,128,1]{3,2,1,0:T(8,128)S(1)} %get-tuple-element.185), channel_id=1, source_target_pairs={{0,64},{64,128},{128,192},{192,256},{256,320},{320,384},{384,448},... | collective-permute-start | bytes 6152 | tf_op jit(solution)/shard_map/while/body/eval_jaxpr/ppermute | solution.py:26
  447.8 6.0 %collective-permute-start.6 = (f32[4,1,1,130]{3,2,1,0:T(1,128)S(1)}, f32[4,1,1,130]{3,2,1,0:T(1,128)S(1)}, u32[]{:S(2)}, u32[]{:S(2)}) collective-permute-start(f32[4,1,1,130]{3,2,1,0:T(1,128)S(1)} %get-tuple-element.186), channel_id=1, source_target_pairs={{0,8},{8,16},{16,24},{24,32},{32,40},{40,48},{48,56},{56,0},{1,9},... | collective-permute-start | bytes 6248 | tf_op jit(solution)/shard_map/while/body/eval_jaxpr/ppermute | solution.py:26
  449.7 6.7 %collective-permute-start.7 = (f32[4,1,1,130]{3,2,1,0:T(1,128)S(1)}, f32[4,1,1,130]{3,2,1,0:T(1,128)S(1)}, u32[]{:S(2)}, u32[]{:S(2)}) collective-permute-start(f32[4,1,1,130]{3,2,1,0:T(1,128)S(1)} %get-tuple-element.187), channel_id=1, source_target_pairs={{8,0},{16,8},{24,16},{32,24},{40,32},{48,40},{56,48},{0,56},{9,1},... | collective-permute-start | bytes 6248 | tf_op jit(solution)/shard_map/while/body/eval_jaxpr/ppermute | solution.py:29
  457.0 7.0 %collective-permute-start.5 = (f32[4,1,128,1]{3,2,1,0:T(8,128)S(1)}, f32[4,1,128,1]{3,2,1,0:T(8,128)S(1)}, u32[]{:S(2)}, u32[]{:S(2)}) collective-permute-start(f32[4,1,128,1]{3,2,1,0:T(8,128)S(1)} %get-tuple-element.185), channel_id=1, source_target_pairs={{0,64},{64,128},{128,192},{192,256},{256,320},{320,384},{384,448},... | collective-permute-start | bytes 6152 | tf_op jit(solution)/shard_map/while/body/eval_jaxpr/ppermute | solution.py:26
  464.2 6.0 %collective-permute-start.6 = (f32[4,1,1,130]{3,2,1,0:T(1,128)S(1)}, f32[4,1,1,130]{3,2,1,0:T(1,128)S(1)}, u32[]{:S(2)}, u32[]{:S(2)}) collective-permute-start(f32[4,1,1,130]{3,2,1,0:T(1,128)S(1)} %get-tuple-element.186), channel_id=1, source_target_pairs={{0,8},{8,16},{16,24},{24,32},{32,40},{40,48},{48,56},{56,0},{1,9},... | collective-permute-start | bytes 6248 | tf_op jit(solution)/shard_map/while/body/eval_jaxpr/ppermute | solution.py:26
  466.1 6.7 %collective-permute-start.7 = (f32[4,1,1,130]{3,2,1,0:T(1,128)S(1)}, f32[4,1,1,130]{3,2,1,0:T(1,128)S(1)}, u32[]{:S(2)}, u32[]{:S(2)}) collective-permute-start(f32[4,1,1,130]{3,2,1,0:T(1,128)S(1)} %get-tuple-element.187), channel_id=1, source_target_pairs={{8,0},{16,8},{24,16},{32,24},{40,32},{48,40},{56,48},{0,56},{9,1},... | collective-permute-start | bytes 6248 | tf_op jit(solution)/shard_map/while/body/eval_jaxpr/ppermute | solution.py:29
  473.4 7.0 %collective-permute-start.5 = (f32[4,1,128,1]{3,2,1,0:T(8,128)S(1)}, f32[4,1,128,1]{3,2,1,0:T(8,128)S(1)}, u32[]{:S(2)}, u32[]{:S(2)}) collective-permute-start(f32[4,1,128,1]{3,2,1,0:T(8,128)S(1)} %get-tuple-element.185), channel_id=1, source_target_pairs={{0,64},{64,128},{128,192},{192,256},{256,320},{320,384},{384,448},... | collective-permute-start | bytes 6152 | tf_op jit(solution)/shard_map/while/body/eval_jaxpr/ppermute | solution.py:26
  480.5 6.0 %collective-permute-start.6 = (f32[4,1,1,130]{3,2,1,0:T(1,128)S(1)}, f32[4,1,1,130]{3,2,1,0:T(1,128)S(1)}, u32[]{:S(2)}, u32[]{:S(2)}) collective-permute-start(f32[4,1,1,130]{3,2,1,0:T(1,128)S(1)} %get-tuple-element.186), channel_id=1, source_target_pairs={{0,8},{8,16},{16,24},{24,32},{32,40},{40,48},{48,56},{56,0},{1,9},... | collective-permute-start | bytes 6248 | tf_op jit(solution)/shard_map/while/body/eval_jaxpr/ppermute | solution.py:26
  482.5 6.7 %collective-permute-start.7 = (f32[4,1,1,130]{3,2,1,0:T(1,128)S(1)}, f32[4,1,1,130]{3,2,1,0:T(1,128)S(1)}, u32[]{:S(2)}, u32[]{:S(2)}) collective-permute-start(f32[4,1,1,130]{3,2,1,0:T(1,128)S(1)} %get-tuple-element.187), channel_id=1, source_target_pairs={{8,0},{16,8},{24,16},{32,24},{40,32},{48,40},{56,48},{0,56},{9,1},... | collective-permute-start | bytes 6248 | tf_op jit(solution)/shard_map/while/body/eval_jaxpr/ppermute | solution.py:29
  489.8 7.0 %collective-permute-start.5 = (f32[4,1,128,1]{3,2,1,0:T(8,128)S(1)}, f32[4,1,128,1]{3,2,1,0:T(8,128)S(1)}, u32[]{:S(2)}, u32[]{:S(2)}) collective-permute-start(f32[4,1,128,1]{3,2,1,0:T(8,128)S(1)} %get-tuple-element.185), channel_id=1, source_target_pairs={{0,64},{64,128},{128,192},{192,256},{256,320},{320,384},{384,448},... | collective-permute-start | bytes 6152 | tf_op jit(solution)/shard_map/while/body/eval_jaxpr/ppermute | solution.py:26
  496.9 6.0 %collective-permute-start.6 = (f32[4,1,1,130]{3,2,1,0:T(1,128)S(1)}, f32[4,1,1,130]{3,2,1,0:T(1,128)S(1)}, u32[]{:S(2)}, u32[]{:S(2)}) collective-permute-start(f32[4,1,1,130]{3,2,1,0:T(1,128)S(1)} %get-tuple-element.186), channel_id=1, source_target_pairs={{0,8},{8,16},{16,24},{24,32},{32,40},{40,48},{48,56},{56,0},{1,9},... | collective-permute-start | bytes 6248 | tf_op jit(solution)/shard_map/while/body/eval_jaxpr/ppermute | solution.py:26
  499.2 6.7 %collective-permute-start.7 = (f32[4,1,1,130]{3,2,1,0:T(1,128)S(1)}, f32[4,1,1,130]{3,2,1,0:T(1,128)S(1)}, u32[]{:S(2)}, u32[]{:S(2)}) collective-permute-start(f32[4,1,1,130]{3,2,1,0:T(1,128)S(1)} %get-tuple-element.187), channel_id=1, source_target_pairs={{8,0},{16,8},{24,16},{32,24},{40,32},{48,40},{56,48},{0,56},{9,1},... | collective-permute-start | bytes 6248 | tf_op jit(solution)/shard_map/while/body/eval_jaxpr/ppermute | solution.py:29
  506.6 7.0 %collective-permute-start.5 = (f32[4,1,128,1]{3,2,1,0:T(8,128)S(1)}, f32[4,1,128,1]{3,2,1,0:T(8,128)S(1)}, u32[]{:S(2)}, u32[]{:S(2)}) collective-permute-start(f32[4,1,128,1]{3,2,1,0:T(8,128)S(1)} %get-tuple-element.185), channel_id=1, source_target_pairs={{0,64},{64,128},{128,192},{192,256},{256,320},{320,384},{384,448},... | collective-permute-start | bytes 6152 | tf_op jit(solution)/shard_map/while/body/eval_jaxpr/ppermute | solution.py:26
  513.7 6.0 %collective-permute-start.6 = (f32[4,1,1,130]{3,2,1,0:T(1,128)S(1)}, f32[4,1,1,130]{3,2,1,0:T(1,128)S(1)}, u32[]{:S(2)}, u32[]{:S(2)}) collective-permute-start(f32[4,1,1,130]{3,2,1,0:T(1,128)S(1)} %get-tuple-element.186), channel_id=1, source_target_pairs={{0,8},{8,16},{16,24},{24,32},{32,40},{40,48},{48,56},{56,0},{1,9},... | collective-permute-start | bytes 6248 | tf_op jit(solution)/shard_map/while/body/eval_jaxpr/ppermute | solution.py:26
  516.4 6.7 %collective-permute-start.7 = (f32[4,1,1,130]{3,2,1,0:T(1,128)S(1)}, f32[4,1,1,130]{3,2,1,0:T(1,128)S(1)}, u32[]{:S(2)}, u32[]{:S(2)}) collective-permute-start(f32[4,1,1,130]{3,2,1,0:T(1,128)S(1)} %get-tuple-element.187), channel_id=1, source_target_pairs={{8,0},{16,8},{24,16},{32,24},{40,32},{48,40},{56,48},{0,56},{9,1},... | collective-permute-start | bytes 6248 | tf_op jit(solution)/shard_map/while/body/eval_jaxpr/ppermute | solution.py:29
  523.7 7.0 %collective-permute-start.5 = (f32[4,1,128,1]{3,2,1,0:T(8,128)S(1)}, f32[4,1,128,1]{3,2,1,0:T(8,128)S(1)}, u32[]{:S(2)}, u32[]{:S(2)}) collective-permute-start(f32[4,1,128,1]{3,2,1,0:T(8,128)S(1)} %get-tuple-element.185), channel_id=1, source_target_pairs={{0,64},{64,128},{128,192},{192,256},{256,320},{320,384},{384,448},... | collective-permute-start | bytes 6152 | tf_op jit(solution)/shard_map/while/body/eval_jaxpr/ppermute | solution.py:26
  530.9 6.0 %collective-permute-start.6 = (f32[4,1,1,130]{3,2,1,0:T(1,128)S(1)}, f32[4,1,1,130]{3,2,1,0:T(1,128)S(1)}, u32[]{:S(2)}, u32[]{:S(2)}) collective-permute-start(f32[4,1,1,130]{3,2,1,0:T(1,128)S(1)} %get-tuple-element.186), channel_id=1, source_target_pairs={{0,8},{8,16},{16,24},{24,32},{32,40},{40,48},{48,56},{56,0},{1,9},... | collective-permute-start | bytes 6248 | tf_op jit(solution)/shard_map/while/body/eval_jaxpr/ppermute | solution.py:26
  533.6 6.7 %collective-permute-start.7 = (f32[4,1,1,130]{3,2,1,0:T(1,128)S(1)}, f32[4,1,1,130]{3,2,1,0:T(1,128)S(1)}, u32[]{:S(2)}, u32[]{:S(2)}) collective-permute-start(f32[4,1,1,130]{3,2,1,0:T(1,128)S(1)} %get-tuple-element.187), channel_id=1, source_target_pairs={{8,0},{16,8},{24,16},{32,24},{40,32},{48,40},{56,48},{0,56},{9,1},... | collective-permute-start | bytes 6248 | tf_op jit(solution)/shard_map/while/body/eval_jaxpr/ppermute | solution.py:29
  540.9 7.0 %collective-permute-start.5 = (f32[4,1,128,1]{3,2,1,0:T(8,128)S(1)}, f32[4,1,128,1]{3,2,1,0:T(8,128)S(1)}, u32[]{:S(2)}, u32[]{:S(2)}) collective-permute-start(f32[4,1,128,1]{3,2,1,0:T(8,128)S(1)} %get-tuple-element.185), channel_id=1, source_target_pairs={{0,64},{64,128},{128,192},{192,256},{256,320},{320,384},{384,448},... | collective-permute-start | bytes 6152 | tf_op jit(solution)/shard_map/while/body/eval_jaxpr/ppermute | solution.py:26
  550.0 6.7 %collective-permute-start.7 = (f32[4,1,1,130]{3,2,1,0:T(1,128)S(1)}, f32[4,1,1,130]{3,2,1,0:T(1,128)S(1)}, u32[]{:S(2)}, u32[]{:S(2)}) collective-permute-start(f32[4,1,1,130]{3,2,1,0:T(1,128)S(1)} %get-tuple-element.187), channel_id=1, source_target_pairs={{8,0},{16,8},{24,16},{32,24},{40,32},{48,40},{56,48},{0,56},{9,1},... | collective-permute-start | bytes 6248 | tf_op jit(solution)/shard_map/while/body/eval_jaxpr/ppermute | solution.py:29
  (26 other events, 520.1 us)
where the time goes:
time: 560 us; the launch traced here: 558 us
  waiting for transfers between devices  209 us (37%)
  starting transfers between devices  152 us (27%)
  blocking collectives  81.8 us (15%)
  other arithmetic  72.5 us (13%)
  local copies, waits for them, and re-layouts  40 us (7%)
    ppermute x40, waiting for transfers between devices, with_halo(): lax.ppermute(lax.slice_in_dim(block, 0, width, axis=dim), axis, backward)  129 us
    ppermute x40, starting transfers between devices, with_halo(): lax.ppermute(lax.slice_in_dim(block, 0, width, axis=dim), axis, backward)  70.6 us
    ppermute x40, waiting for transfers between devices, with_halo(): lax.ppermute(lax.slice_in_dim(block, block.shape[dim] - width, None, axis...  62.8 us
    ppermute x40, starting transfers between devices, with_halo(): lax.ppermute(lax.slice_in_dim(block, block.shape[dim] - width, None, axis...  57.2 us
    scatter-add x2, other arithmetic, per_device(): adjoint_slab.at[index_low].add(amount_low).at[index_high].add(amount_high)  44.9 us
    all_gather x1, blocking collectives, per_device(): columns = lax.all_gather(slab, 'obs', axis=1, tiled=True)  29.7 us
    all_gather x1, blocking collectives, per_device(): targets = lax.all_gather(lower_index, 'obs', axis=0, tiled=True)  27.4 us
    all_gather x1, blocking collectives, per_device(): lax.all_gather(jnp.stack([lower_share, upper_share]), 'obs', axis=1, tile...  24.7 us
  transfers between devices with their start and end apart: 85, of which 62 were waited for; matrix products, arithmetic and copies ran while one was open for 3% of the time, Pallas kernels for 0%

commit v1 on v0

v1 whole, which is shorter than its diff:
```python
import jax
import jax.numpy as jnp
from jax import lax
from jax.experimental import pallas as pl
from jax.experimental.pallas import tpu as pltpu
from jax.sharding import PartitionSpec as P

STEPS = 10
HALO = STEPS
ROWS = 16
PITCH = 2 * HALO
PAD = 8
F32, BF16, I32 = jnp.float32, jnp.bfloat16, jnp.int32


def lanes(shape):
    return lax.broadcasted_iota(I32, shape, len(shape) - 1)


def subs(shape):
    return lax.broadcasted_iota(I32, shape, len(shape) - 2)


def split3(x):
    hi = x.astype(BF16)
    rest = x - hi.astype(F32)
    mid = rest.astype(BF16)
    low = (rest - mid.astype(F32)).astype(BF16)
    return hi, mid, low


def one_hot(flags):
    return jnp.where(flags, 1.0, 0.0).astype(BF16)


def dot_nn(a, b):
    return lax.dot_general(a, b, (((1,), (0,)), ((), ())), preferred_element_type=F32)


def dot_nt(a, b):
    return lax.dot_general(a, b, (((1,), (1,)), ((), ())), preferred_element_type=F32)


def call(body, outs, args, scratch=(), flops=1_000_000, smem=()):
    vmem = pl.BlockSpec(memory_space=pltpu.VMEM)
    moved = sum(a.size * 4 for a in args) + sum(4 * _size(s) for s in outs)
    return pl.pallas_call(
        body,
        out_shape=[jax.ShapeDtypeStruct(s, F32) for s in outs],
        in_specs=[vmem] * len(args),
        out_specs=[vmem] * len(outs),
        scratch_shapes=list(scratch),
        cost_estimate=pl.CostEstimate(flops=flops, bytes_accessed=moved, transcendentals=0),
        name=body.__name__,
    )(*args)


def _size(shape):
    n = 1
    for s in shape:
        n *= s
    return n


def masked_north(rate_ref):
    north = rate_ref[1]
    top = lax.axis_index("gy") == lax.axis_size("gy") - 1
    return jnp.where(top & (subs(north.shape) == north.shape[0] - 1), 0.0, north)


def pack_edges(arrays, east_ref, west_ref):
    lane = lanes(arrays[0].shape)
    east = jnp.zeros(arrays[0].shape, F32)
    west = jnp.zeros(arrays[0].shape, F32)
    for a, x in enumerate(arrays):
        width = x.shape[-1]
        low = a * PITCH + HALO
        moved = pltpu.roll(x, (low - (width - HALO)) % width, 1)
        east = jnp.where((lane >= low) & (lane < low + HALO), moved, east)
        low = a * PITCH
        moved = pltpu.roll(x, low % width, 1) if low else x
        west = jnp.where((lane >= low) & (lane < low + HALO), moved, west)
    east_ref[...] = east
    west_ref[...] = west


def pack_inputs(ctl, rate, prof, field, level, weight, innov, prec, east, west, obs):
    pack_edges([ctl[f] for f in range(ctl.shape[0])] + [rate[0], masked_north(rate)], east, west)
    index = ((field[...] * 8 + level[...]) * 512 + prof[...]).astype(F32)
    rows = jnp.concatenate([index, weight[...], innov[...], prec[...]], axis=0)
    for z in range(obs.shape[0] // rows.shape[0]):
        obs[pl.ds(z * rows.shape[0], rows.shape[0]), :] = rows


def north_south(arrays, strip, north_ref, south_ref):
    for a, x in enumerate(arrays + [strip]):
        north_ref[a] = x[x.shape[0] - ROWS :]
        south_ref[a] = x[:ROWS]


def edges_first(ctl, rate, left, right, strip, north, south):
    joined = left[...] + right[...]
    strip[...] = joined
    arrays = [ctl[f] for f in range(ctl.shape[0])] + [rate[0], masked_north(rate)]
    north_south(arrays, joined, north, south)


def edges_second(pulled, left, right, strip, north, south):
    joined = left[...] + right[...]
    strip[...] = joined
    north_south([pulled[f] for f in range(pulled.shape[0])], joined, north, south)


def unpack(block, a):
    width = block.shape[-1]
    east = pltpu.roll(block, (-a * PITCH) % width, 1) if a else block
    west = pltpu.roll(block, (width - HALO - a * PITCH - HALO) % width, 1)
    return jnp.where(lanes(block.shape) < width // 2, east, west)


def blocks(own, south, north):
    height = own.shape[0]
    return ((PAD, south), (PAD + ROWS, own), (PAD + ROWS + height, north))


def turned(main, beyond, by):
    width = main.shape[-1]
    edge = lanes(main.shape) == (0 if by == 1 else width - 1)
    a = pltpu.roll(main, by % width, 1)
    b = pltpu.roll(beyond, by % width, 1)
    return jnp.where(edge, b, a), jnp.where(edge, a, b)


def one_step(source, coef, store, first, last):
    fields = source.shape[0] // 2
    for tile in range(first, last):
        row = PAD + 8 * tile
        here, up, down = pl.ds(row, 8), pl.ds(row + 1, 8), pl.ds(row - 1, 8)
        c = [coef[i, pl.ds(8 * tile, 8), :] for i in range(10)]
        for f in range(fields):
            m, s = source[2 * f, here, :], source[2 * f + 1, here, :]
            me, se = turned(m, s, -1)
            mw, sw = turned(m, s, 1)
            new_m = c[0] * m + c[2] * me + c[4] * mw + c[6] * source[2 * f, up, :]
            new_m = new_m + c[8] * source[2 * f, down, :]
            new_s = c[1] * s + c[3] * se + c[5] * sw + c[7] * source[2 * f + 1, up, :]
            new_s = new_s + c[9] * source[2 * f + 1, down, :]
            store(f, tile, new_m, new_s)


def ten_steps(a, b, coef, finish, tiles):
    def into(target):
        def store(f, tile, main, beyond):
            target[2 * f, pl.ds(PAD + 8 * tile, 8), :] = main
            target[2 * f + 1, pl.ds(PAD + 8 * tile, 8), :] = beyond

        return store

    one_step(a, coef, into(b), 0, tiles)

    def body(_, carry):
        one_step(b, coef, into(a), 1, tiles - 1)
        one_step(a, coef, into(b), 1, tiles - 1)
        return carry

    lax.fori_loop(0, STEPS // 2 - 1, body, 0)

    def store(f, tile, main, beyond):
        finish(f, 8 * tile - ROWS, main)

    one_step(b, coef, store, ROWS // 8, tiles - ROWS // 8)


def load_field(a, own, strip, south, north):
    fields = own.shape[0]
    for f in range(fields):
        for row, block in blocks(own[f], south[f], north[f]):
            a[2 * f, pl.ds(row, block.shape[0]), :] = block
    for row, block in blocks(strip[...], south[south.shape[0] - 1], north[north.shape[0] - 1]):
        for f in range(fields):
            a[2 * f + 1, pl.ds(row, block.shape[0]), :] = unpack(block, f)
    clear = jnp.zeros((PAD, a.shape[2]), F32)
    for plane in range(a.shape[0]):
        a[plane, pl.ds(0, PAD), :] = clear
        a[plane, pl.ds(a.shape[1] - PAD, PAD), :] = clear


def diffuse_control(ctl, rate, strip, south, north, inc, coef, a, b, rates):
    fields = ctl.shape[0]
    tiles = coef.shape[1] // 8
    own_rates = (rate[0], masked_north(rate))
    for k in range(2):
        for row, block in blocks(own_rates[k], south[fields + k], north[fields + k]):
            rates[2 * k, pl.ds(row, block.shape[0]), :] = block
        for row, block in blocks(strip[...], south[fields + 2], north[fields + 2]):
            lane = lanes(block.shape)
            near = (lane < HALO) | (lane >= block.shape[-1] - HALO)
            rates[2 * k + 1, pl.ds(row, block.shape[0]), :] = jnp.where(
                near, unpack(block, fields + k), 0.0
            )
        clear = jnp.zeros((PAD, rates.shape[2]), F32)
        for plane in (2 * k, 2 * k + 1):
            rates[plane, pl.ds(0, PAD), :] = clear
    for tile in range(tiles):
        here, down = pl.ds(PAD + 8 * tile, 8), pl.ds(PAD + 8 * tile - 1, 8)
        east = (rates[0, here, :], rates[1, here, :])
        west = turned(east[0], east[1], 1)
        for plane in range(2):
            n, s = rates[2 + plane, here, :], rates[2 + plane, down, :]
            e, w = east[plane], west[plane]
            for i, value in enumerate((1.0 - e - w - n - s, e, w, n, s)):
                coef[2 * i + plane, pl.ds(8 * tile, 8), :] = value
    load_field(a, ctl, strip, south, north)

    def finish(f, row, main):
        inc[f, pl.ds(row, 8), :] = main

    ten_steps(a, b, coef, finish, tiles)


def diffuse_pulled(pulled, strip, south, north, coef, ctl, grad, a, b):
    load_field(a, pulled, strip, south, north)

    def finish(f, row, main):
        grad[f, pl.ds(row, 8), :] = ctl[f, pl.ds(row, 8), :] + main

    ten_steps(a, b, coef, finish, coef.shape[1] // 8)


def tables(obs, holder, cell, out, slots):
    profiles = holder.shape[1]
    level_here = lax.axis_index("obs")
    groups = obs.shape[0] // 16
    width = obs.shape[1]
    acc = jnp.zeros((48, profiles), F32)
    row16 = subs((16, width))
    for z in range(groups):
        parts = ([], [], [])
        hots = []
        for c in range(4):
            at = 16 * z + c
            index = obs[pl.ds(at, 1), :].astype(I32)
            w, y, q = (obs[pl.ds(at + 4 * k, 1), :] for k in (1, 2, 3))
            prof = index & 511
            level = (index >> 9) & 7
            field = index >> 12
            low = jnp.where(level == level_here, q, 0.0)
            high = jnp.where(level == level_here - 1, q, 0.0)
            v = 1.0 - w
            lw, hv = low * w, high * v
            rows = (lw * w + hv * v, lw * v, hv * w, (lw + hv) * y)
            value = jnp.where(
                row16 < 8,
                jnp.where(row16 < 4, rows[0], rows[1]),
                jnp.where(row16 < 12, rows[2], rows[3]),
            )
            value = jnp.where((row16 & 3) == field, value, 0.0)
            for part, x in zip(parts, split3(value)):
                part.append(x)
            hots.append(one_hot(subs((profiles, width)) == prof))
        left = jnp.concatenate([jnp.concatenate(p, axis=1) for p in parts], axis=0)
        acc = acc + dot_nt(left, jnp.concatenate(hots, axis=1))
    table = acc[0:16] + acc[16:32] + acc[32:48]
    held = subs((out.shape[0], profiles)) == holder[...]
    held16 = one_hot(held)
    before = one_hot(subs((profiles, profiles)) < lanes((profiles, profiles)))
    slot = jnp.sum(jnp.where(held, dot_nn(held16, before), 0.0), axis=0, keepdims=True)
    slots[...] = slot
    place = slot.astype(I32)
    cells = cell[...].astype(F32)
    mine = [subs((8, profiles)) * 2 + k == place for k in range(2)]
    for k in range(2):
        value = jnp.concatenate(
            [jnp.where(mine[k], table[r : r + 1], 0.0) for r in range(16)], axis=0
        )
        total = sum(dot_nt(held16, part) for part in split3(value))
        out[:, k, :] = total
    value = jnp.concatenate(
        [jnp.where(mine[k], cells, 0.0) for k in range(2)]
        + [jnp.zeros((112, profiles), F32)],
        axis=0,
    )
    out[:, 2, :] = sum(dot_nt(held16, part) for part in split3(value)[:2])


def gather(inc, sent, found, tab, hold):
    fields = inc.shape[0]
    tab[pl.ds(0, 128), :] = jnp.concatenate([sent[:, 0, :], sent[:, 1, :]], axis=0).T
    cells = jnp.concatenate([sent[:, 2, :], sent[:, 2, :]], axis=0).T
    cells = jnp.where(lanes((8, 128)) < 64, cells[0:8], cells[8:16])
    tab[pl.ds(128, 8), :] = cells
    cells = cells.astype(I32)
    left = jnp.concatenate(
        [jnp.concatenate(split3(inc[f]), axis=1) for f in range(fields)], axis=0
    )
    for pair in range(4):
        hots, lats = [], []
        for s in (2 * pair, 2 * pair + 1):
            row = cells[s : s + 1]
            hots.append(one_hot(subs((128, 128)) == (row & 127)))
            lats.append(subs((128, 128)) == (row >> 7))
        hot = jnp.concatenate(hots, axis=1)
        hit = dot_nn(left, jnp.concatenate([hot, hot, hot], axis=0))
        for f in range(fields):
            for i in range(2):
                part = hit[128 * f : 128 * (f + 1), 128 * i : 128 * (i + 1)]
                hold[pl.ds(8 * f + 2 * pair + i, 1), :] = jnp.sum(
                    jnp.where(lats[i], part, 0.0), axis=0, keepdims=True
                )
    rows = hold[...]
    for z in range(found.shape[0] // rows.shape[0]):
        found[pl.ds(z * rows.shape[0], rows.shape[0]), :] = rows


def scatter(levels, tab, pulled, east, west, columns):
    fields = pulled.shape[0]
    rows = 8 * fields
    here = lax.axis_index("obs")
    top = levels.shape[0] // rows - 1

    def level(k):
        return levels[pl.ds(pl.multiple_of(jnp.clip(k, 0, top) * rows, rows), rows), :]

    own, above, below = level(here), level(here + 1), level(here - 1)
    d, o, u, b = (tab[pl.ds(rows * k, rows), :] for k in range(4))
    amount = d * own + o * above + u * below - b
    cells = tab[pl.ds(4 * rows, 8), :].astype(I32)
    lat = [subs((128, 128)) == (cells[s : s + 1] >> 7) for s in range(8)]
    hot = jnp.concatenate(
        [one_hot(subs((128, 128)) == (cells[s : s + 1] & 127)) for s in range(8)], axis=1
    )
    for f in range(fields):
        total = jnp.zeros((128, 128), F32)
        for part in split3(amount[8 * f : 8 * f + 8]):
            wide = part.astype(F32)
            left = jnp.concatenate(
                [jnp.where(lat[s], wide[s : s + 1], 0.0).astype(BF16) for s in range(8)], axis=1
            )
            total = total + dot_nt(left, hot)
        pulled[f] = total
    pack_edges([pulled[f] for f in range(fields)], east, west)
    for half in range(2):
        turned_block = levels[pl.ds(128 * half, 128), :].T
        for k in range(2):
            columns[:, 2 * k + half, :] = turned_block[64 * k : 64 * (k + 1)]


def depart(columns, holder, slots, prof, field, level, weight, innov, prec, out):
    profiles = holder.shape[1]
    left = jnp.concatenate(
        [
            jnp.concatenate([columns[:, half, :], columns[:, 2 + half, :]], axis=0).T
            for half in range(2)
        ],
        axis=0,
    )
    place = slots[...].astype(I32)
    row = subs((128, profiles))
    held = one_hot(((row & 63) == holder[...]) & ((row >> 6) == (place & 1)))
    spread = dot_nn(
        jnp.concatenate(split3(left), axis=1), jnp.concatenate([held, held, held], axis=0)
    )
    mine = subs((8, profiles)) == (place >> 1)
    values = jnp.concatenate(
        [
            jnp.sum(jnp.where(mine, spread[8 * r : 8 * r + 8], 0.0), axis=0, keepdims=True)
            for r in range(32)
        ],
        axis=0,
    )
    hot = jnp.concatenate(
        [one_hot(subs((profiles, 128)) == prof[pl.ds(c, 1), :]) for c in range(4)], axis=1
    )
    seen = sum(dot_nn(part, hot) for part in split3(values))
    row = subs((32, 128))
    for c in range(4):
        at = pl.ds(c, 1)
        code = level[at, :] * 4 + field[at, :]
        part = seen[:, 128 * c : 128 * (c + 1)]
        low = jnp.sum(jnp.where(row == code, part, 0.0), axis=0, keepdims=True)
        high = jnp.sum(jnp.where(row == code + 4, part, 0.0), axis=0, keepdims=True)
        w = weight[at, :]
        out[at, :] = prec[at, :] * (w * low + (1.0 - w) * high - innov[at, :])


def ring(axis, by):
    count = lax.axis_size(axis)
    return [(i, (i + by) % count) for i in range(count)]


def pair(forward, back, axis):
    return (
        lax.ppermute(forward, axis, ring(axis, 1)),
        lax.ppermute(back, axis, ring(axis, -1)),
    )


def per_device(
    control,
    diffusivity,
    prof_tile,
    prof_cell,
    obs_prof,
    obs_field,
    obs_level,
    obs_weight,
    innovation,
    obs_precision,
):
    fields, _, ny, nx = control.shape
    tile = (ny, nx)
    profiles = prof_tile.shape[0]
    holders = lax.axis_size("gx") * lax.axis_size("gy")
    levels = lax.axis_size("obs")
    ext = ny + 2 * ROWS
    ctl = control.reshape(fields, ny, nx)
    rate = diffusivity.reshape(2, ny, nx)
    holder = prof_tile.reshape(1, profiles)
    cell = prof_cell.reshape(1, profiles)
    obs = [
        x.reshape(4, 128)
        for x in (obs_prof, obs_field, obs_level, obs_weight, innovation, obs_precision)
    ]
    planes = pltpu.VMEM((2 * fields, ext + 2 * PAD, nx), F32)

    east, west, rows = call(pack_inputs, [tile, tile, (levels * 16, 128)], [ctl, rate, *obs])
    rows = lax.all_to_all(rows, "obs", 0, 0, tiled=True)
    left, right = pair(east, west, "gx")
    side = (fields + 3, ROWS, nx)
    strip, north, south = call(edges_first, [tile, side, side], [ctl, rate, left, right])
    south, north = pair(north, south, "gy")
    table, slots = call(
        tables, [(holders, 3, 128), (1, profiles)], [rows, holder, cell], flops=400_000_000
    )
    table = lax.all_to_all(table, ("gx", "gy"), 0, 0, tiled=True)
    inc, coef = call(
        diffuse_control,
        [(fields, ny, nx), (10, ext, nx)],
        [ctl, rate, strip, south, north],
        [planes, planes, pltpu.VMEM((4, ext + 2 * PAD, nx), F32)],
        flops=40_000_000,
    )
    found, tab = call(
        gather,
        [(levels * fields * 8, 128), (136, 128)],
        [inc, table],
        [pltpu.VMEM((fields * 8, 128), F32)],
        flops=400_000_000,
    )
    found = lax.all_to_all(found, "obs", 0, 0, tiled=True)
    pulled, east, west, columns = call(
        scatter,
        [(fields, ny, nx), tile, tile, (holders, 4, 128)],
        [found, tab],
        flops=400_000_000,
    )
    left, right = pair(east, west, "gx")
    columns = lax.all_to_all(columns, ("gx", "gy"), 0, 0, tiled=True)
    side = (fields + 1, ROWS, nx)
    strip, north, south = call(edges_second, [tile, side, side], [pulled, left, right])
    south, north = pair(north, south, "gy")
    (gradient,) = call(
        diffuse_pulled,
        [(fields, ny, nx)],
        [pulled, strip, south, north, coef, ctl],
        [planes, planes],
        flops=40_000_000,
    )
    (departures,) = call(depart, [(4, 128)], [columns, holder, slots, *obs], flops=400_000_000)
    return gradient.reshape(control.shape), departures.reshape(obs_prof.shape)


def solution(mesh):
    in_specs = (
        P(None, "obs", "gy", "gx"),
        P(None, "obs", "gy", "gx"),
        P(("gx", "gy"), None),
        P(("gx", "gy")),
        P(("gx", "gy", "obs")),
        P(("gx", "gy", "obs")),
        P(("gx", "gy", "obs")),
        P(("gx", "gy", "obs")),
        P(("gx", "gy", "obs")),
        P(("gx", "gy", "obs")),
    )
    out_specs = (P(None, "obs", "gy", "gx"), P(("gx", "gy", "obs")))
    return jax.shard_map(
        per_device, mesh=mesh, in_specs=in_specs, out_specs=out_specs, check_vma=False
    )
```

time: 560 us -> 118 us (0.21)
  the two profiles are of different devices: /device:TPU:56 before, /device:TPU:24 now
where the time goes in v1:
time: 118 us; the launch traced here: 117 us
  starting transfers between devices  36.9 us (31%)
  blocking collectives  31.8 us (27%)
  Pallas kernels  27.6 us (23%)
  waiting for transfers between devices  15.5 us (13%)
  local copies, waits for them, and re-layouts  4.44 us (4%)
    pallas_call x9, Pallas kernels, call(): pl.pallas_call(body, out_shape=[jax.ShapeDtypeStruct(s, F32) for s in out...  27.6 us
    all_to_all x1, blocking collectives, per_device(): rows = lax.all_to_all(rows, 'obs', 0, 0, tiled=True)  18.8 us
    all_to_all x1, blocking collectives, per_device(): found = lax.all_to_all(found, 'obs', 0, 0, tiled=True)  13.1 us
    ppermute x4, waiting for transfers between devices, pair(): lax.ppermute(back, axis, ring(axis, -1))  10.7 us
    all_to_all x1, starting transfers between devices, per_device(): table = lax.all_to_all(table, ('gx', 'gy'), 0, 0, tiled=True)  10.5 us
    ppermute x4, starting transfers between devices, pair(): lax.ppermute(forward, axis, ring(axis, 1))  10 us
    ppermute x4, starting transfers between devices, pair(): lax.ppermute(back, axis, ring(axis, -1))  9.51 us
    all_to_all x1, starting transfers between devices, per_device(): columns = lax.all_to_all(columns, ('gx', 'gy'), 0, 0, tiled=True)  6.95 us
  transfers between devices with their start and end apart: 10, of which 5 were waited for; matrix products, arithmetic and copies ran while one was open for 0% of the time, Pallas kernels for 12%

profile of v1, /device:TPU:24, one launch (start us, length us, event | category | flops | bytes accessed | tf_op | source)
XLA Modules:
  0.0 117.0 jit_solution(14647139786684759146)
XLA Ops:
  0.6 2.0 %pack_inputs.1 = (f32[128,128]{1,0:T(8,128)}, f32[128,128]{1,0:T(8,128)}, f32[128,128]{1,0:T(8,128)}) custom-call(f32[4,128,128]{2,1,0:T(8,128)} %bitcast.18, f32[2,128,128]{2,1,0:T(8,128)} %bitcast.22, s32[4,128]{1,0:T(4,128)} %bitcast.30, s32[4,128]{1,0:T(4,128)} %bitcast.32, s32[4,128]{1,0:T(4,128)} %bitcast.34, f32[4,128]{1,0:T(4,128)} %bitcast.36, ...), custom_call_target="tpu_custom_call" | custom-call | flops 1000000 | bytes 602112 | tf_op jit(solution)/shard_map/pack_inputs/pallas_call | solution.py:47
  2.6 18.8 %all_to_all.32 = f32[8,16,128]{2,1,0:T(8,128)} all-to-all(f32[8,16,128]{2,1,0:T(8,128)} %bitcast.28), channel_id=1, replica_groups=mesh['gx'=8,'gy'=8,'obs'=8] {'obs'}, dimensions={0} | all-to-all | bytes 131072 | tf_op jit(solution)/shard_map/all_to_all | solution.py:427
  21.4 3.5 %tables.1 = (f32[64,3,128]{2,1,0:T(4,128)}, f32[1,512]{1,0:T(1,128)}) custom-call(f32[128,128]{1,0:T(8,128)} %bitcast.29, s32[1,512]{1,0:T(1,128)} %bitcast.43, s32[1,512]{1,0:T(1,128)} %bitcast.42), custom_call_target="tpu_custom_call" | custom-call | flops 400000000 | bytes 169984 | tf_op jit(solution)/shard_map/tables/pallas_call | solution.py:47
  24.9 0.0 copy-start.12
  24.9 0.0 copy-start.10
  24.9 10.5 %all-to-all-start.1 = ((f32[64,3,128]{2,1,0:T(4,128)}), f32[64,3,128]{2,1,0:T(4,128)S(1)}, u32[]{:S(2)}, u32[]{:S(2)}) async-start(f32[64,3,128]{2,1,0:T(4,128)} %get-tuple-element.28), calls=%async_computation.1 | async-start | bytes 262144 | tf_op jit(solution)/shard_map/all_to_all | solution.py:435
  35.3 0.0 copy-done.12
  35.4 0.1 collective-permute-start
  35.5 0.0 copy-done.10
  35.5 2.8 %collective-permute-start.1 = (f32[128,128]{1,0:T(8,128)S(1)}, f32[128,128]{1,0:T(8,128)S(1)}, u32[]{:S(2)}, u32[]{:S(2)}) collective-permute-start(f32[128,128]{1,0:T(8,128)S(1)} %copy-done.10), channel_id=1, source_target_pairs={{0,448},{64,0},{128,64},{192,128},{256,192},{320,256},{384,320},{4... | collective-permute-start | bytes 196616 | tf_op jit(solution)/shard_map/ppermute | solution.py:394
  38.3 2.3 %collective-permute-done.left = f32[128,128]{1,0:T(8,128)S(1)} collective-permute-done((f32[128,128]{1,0:T(8,128)S(1)}, f32[128,128]{1,0:T(8,128)S(1)}, u32[]{:S(2)}, u32[]{:S(2)}) %collective-permute-start) | collective-permute-done | bytes 65568 | tf_op jit(solution)/shard_map/ppermute | solution.py:393
  40.6 0.0 copy-start.4
  40.6 0.0 collective-permute-done.1.right
  40.6 0.6 copy-done.4
  41.2 0.0 copy-start.5
  41.2 0.6 copy-done.5
  41.9 1.7 %edges_first.1 = (f32[128,128]{1,0:T(8,128)}, f32[7,16,128]{2,1,0:T(8,128)}, f32[7,16,128]{2,1,0:T(8,128)}) custom-call(f32[4,128,128]{2,1,0:T(8,128)} %bitcast.19, f32[2,128,128]{2,1,0:T(8,128)} %bitcast.23, f32[128,128]{1,0:T(8,128)} %copy-done.4, f32[128,128]{1,0:T(8,128)} %copy-done.5), custom_call_target="tpu_custom_call" | custom-call | flops 1000000 | bytes 704512 | tf_op jit(solution)/shard_map/edges_first/pallas_call | solution.py:47
  43.6 4.9 %collective-permute-start.2 = (f32[7,16,128]{2,1,0:T(8,128)}, f32[7,16,128]{2,1,0:T(8,128)S(1)}, u32[]{:S(2)}, u32[]{:S(2)}) collective-permute-start(f32[7,16,128]{2,1,0:T(8,128)} %get-tuple-element.24), channel_id=1, source_target_pairs={{0,8},{8,16},{16,24},{24,32},{32,40},{40,48},{48,56},{56,0},{1,9},... | collective-permute-start | bytes 172040 | tf_op jit(solution)/shard_map/ppermute | solution.py:393
  48.5 1.9 %collective-permute-start.3 = (f32[7,16,128]{2,1,0:T(8,128)}, f32[7,16,128]{2,1,0:T(8,128)S(1)}, u32[]{:S(2)}, u32[]{:S(2)}) collective-permute-start(f32[7,16,128]{2,1,0:T(8,128)} %get-tuple-element.25), channel_id=1, source_target_pairs={{0,56},{8,0},{16,8},{24,16},{32,24},{40,32},{48,40},{56,48},{1,57}... | collective-permute-start | bytes 172040 | tf_op jit(solution)/shard_map/ppermute | solution.py:394
  50.4 0.2 collective-permute-done.2.south
  50.6 0.0 copy-start.6
  50.6 5.4 %collective-permute-done.3.north = f32[7,16,128]{2,1,0:T(8,128)S(1)} collective-permute-done((f32[7,16,128]{2,1,0:T(8,128)}, f32[7,16,128]{2,1,0:T(8,128)S(1)}, u32[]{:S(2)}, u32[]{:S(2)}) %collective-permute-start.3) | collective-permute-done | bytes 57376 | tf_op jit(solution)/shard_map/ppermute | solution.py:394
  55.9 0.0 copy-start.7
  55.9 0.0 copy-done.6
  55.9 0.6 copy-done.7
  56.6 5.4 %diffuse_control.1 = (f32[4,128,128]{2,1,0:T(8,128)}, f32[10,160,128]{2,1,0:T(8,128)}) custom-call(f32[4,128,128]{2,1,0:T(8,128)} %bitcast.20, f32[2,128,128]{2,1,0:T(8,128)} %bitcast.24, f32[128,128]{1,0:T(8,128)} %get-tuple-element.23.strip, f32[7,16,128]{2,1,0:T(8,128)} %copy-done.6, f32[7,16,128]{2,1,0:T(8,128)} %copy-done.7), custom_call_target="tpu_custom_call" | custom-call | flops 40000000 | bytes 1654784 | tf_op jit(solution)/shard_map/diffuse_control/pallas_call | solution.py:47
  62.0 0.0 all-to-all-done.1.sent
  62.0 0.0 copy-start.1
  62.0 0.6 copy-done.1
  62.7 2.5 %gather.1 = (f32[256,128]{1,0:T(8,128)}, f32[136,128]{1,0:T(8,128)}) custom-call(f32[4,128,128]{2,1,0:T(8,128)} %get-tuple-element.26.inc, f32[64,3,128]{2,1,0:T(4,128)} %copy-done.1), custom_call_target="tpu_custom_call" | custom-call | flops 400000000 | bytes 561152 | tf_op jit(solution)/shard_map/gather/pallas_call | solution.py:47
  65.2 13.1 %all_to_all.33 = f32[8,32,128]{2,1,0:T(8,128)} all-to-all(f32[8,32,128]{2,1,0:T(8,128)} %bitcast.27), channel_id=1, replica_groups=mesh['gx'=8,'gy'=8,'obs'=8] {'obs'}, dimensions={0} | all-to-all | bytes 262144 | tf_op jit(solution)/shard_map/all_to_all | solution.py:450
  78.2 2.8 %scatter.1 = (f32[4,128,128]{2,1,0:T(8,128)}, f32[128,128]{1,0:T(8,128)}, f32[128,128]{1,0:T(8,128)}, f32[64,4,128]{2,1,0:T(4,128)}) custom-call(f32[256,128]{1,0:T(8,128)} %bitcast.26, f32[136,128]{1,0:T(8,128)} %get-tuple-element.30.tab), custom_call_target="tpu_custom_call" | custom-call | flops 400000000 | bytes 724992 | tf_op jit(solution)/shard_map/scatter/pallas_call | solution.py:47
  81.0 0.0 copy-start.13
  81.0 0.0 copy-start.11
  81.0 6.9 %all-to-all-start.3 = ((f32[64,4,128]{2,1,0:T(4,128)}), f32[64,4,128]{2,1,0:T(4,128)S(1)}, u32[]{:S(2)}, u32[]{:S(2)}) async-start(f32[64,4,128]{2,1,0:T(4,128)} %get-tuple-element.38), calls=%async_computation.3 | async-start | bytes 262144 | tf_op jit(solution)/shard_map/all_to_all | solution.py:458
  88.0 0.0 copy-done.13
  88.0 0.1 collective-permute-start.4
  88.1 0.0 copy-done.11
  88.1 2.8 %collective-permute-start.5 = (f32[128,128]{1,0:T(8,128)S(1)}, f32[128,128]{1,0:T(8,128)S(1)}, u32[]{:S(2)}, u32[]{:S(2)}) collective-permute-start(f32[128,128]{1,0:T(8,128)S(1)} %copy-done.11), channel_id=1, source_target_pairs={{0,448},{64,0},{128,64},{192,128},{256,192},{320,256},{384,320},{4... | collective-permute-start | bytes 196616 | tf_op jit(solution)/shard_map/ppermute | solution.py:394
  90.9 2.3 %collective-permute-done.4.left = f32[128,128]{1,0:T(8,128)S(1)} collective-permute-done((f32[128,128]{1,0:T(8,128)S(1)}, f32[128,128]{1,0:T(8,128)S(1)}, u32[]{:S(2)}, u32[]{:S(2)}) %collective-permute-start.4) | collective-permute-done | bytes 65568 | tf_op jit(solution)/shard_map/ppermute | solution.py:393
  93.2 0.0 copy-start.2
  93.2 0.0 collective-permute-done.5.right
  93.2 0.0 copy-start.3
  93.2 0.6 copy-done.2
  93.8 0.0 copy-done.3
  93.9 1.7 %edges_second.1 = (f32[128,128]{1,0:T(8,128)}, f32[5,16,128]{2,1,0:T(8,128)}, f32[5,16,128]{2,1,0:T(8,128)}) custom-call(f32[4,128,128]{2,1,0:T(8,128)} %get-tuple-element.31.pulled, f32[128,128]{1,0:T(8,128)} %copy-done.2, f32[128,128]{1,0:T(8,128)} %copy-done.3), custom_call_target="tpu_custom_call" | custom-call | flops 1000000 | bytes 540672 | tf_op jit(solution)/shard_map/edges_second/pallas_call | solution.py:47
  95.5 4.9 %collective-permute-start.6 = (f32[5,16,128]{2,1,0:T(8,128)}, f32[5,16,128]{2,1,0:T(8,128)S(1)}, u32[]{:S(2)}, u32[]{:S(2)}) collective-permute-start(f32[5,16,128]{2,1,0:T(8,128)} %get-tuple-element.35), channel_id=1, source_target_pairs={{0,8},{8,16},{16,24},{24,32},{32,40},{40,48},{48,56},{56,0},{1,9},... | collective-permute-start | bytes 122888 | tf_op jit(solution)/shard_map/ppermute | solution.py:393
  100.4 1.9 %collective-permute-start.7 = (f32[5,16,128]{2,1,0:T(8,128)}, f32[5,16,128]{2,1,0:T(8,128)S(1)}, u32[]{:S(2)}, u32[]{:S(2)}) collective-permute-start(f32[5,16,128]{2,1,0:T(8,128)} %get-tuple-element.36), channel_id=1, source_target_pairs={{0,56},{8,0},{16,8},{24,16},{32,24},{40,32},{48,40},{56,48},{1,57}... | collective-permute-start | bytes 122888 | tf_op jit(solution)/shard_map/ppermute | solution.py:394
  102.3 0.0 collective-permute-done.6.south
  102.4 0.0 copy-start.8
  102.4 5.3 %collective-permute-done.7.north = f32[5,16,128]{2,1,0:T(8,128)S(1)} collective-permute-done((f32[5,16,128]{2,1,0:T(8,128)}, f32[5,16,128]{2,1,0:T(8,128)S(1)}, u32[]{:S(2)}, u32[]{:S(2)}) %collective-permute-start.7) | collective-permute-done | bytes 40992 | tf_op jit(solution)/shard_map/ppermute | solution.py:394
  107.7 0.0 copy-start.9
  107.7 0.0 copy-done.8
  107.7 0.6 copy-done.9
  108.3 5.6 %diffuse_pulled.1 = f32[4,128,128]{2,1,0:T(8,128)} custom-call(f32[4,128,128]{2,1,0:T(8,128)} %get-tuple-element.31.pulled, f32[128,128]{1,0:T(8,128)} %get-tuple-element.34.strip, f32[5,16,128]{2,1,0:T(8,128)} %copy-done.8, f32[5,16,128]{2,1,0:T(8,128)} %copy-done.9, f32[10,160,128]{2,1,0:T(8,128)} %get-tuple-element.37.coef, f32[4,128,128]{2,1,0:T(8,128)} %bitcast.21), custom_call_target="tpu_custom_call" | custom-call | flops 40000000 | bytes 1753088 | tf_op jit(solution)/shard_map/diffuse_pulled/pallas_call | solution.py:47
  114.0 0.0 all-to-all-done.3.columns
  114.0 0.0 copy-start
  114.0 0.7 copy-done
  114.6 2.4 %depart.1 = f32[4,128]{1,0:T(4,128)} custom-call(f32[64,4,128]{2,1,0:T(4,128)} %copy-done, s32[1,512]{1,0:T(1,128)} %bitcast.44, f32[1,512]{1,0:T(1,128)} %get-tuple-element.39.slots, s32[4,128]{1,0:T(4,128)} %bitcast.31, s32[4,128]{1,0:T(4,128)} %bitcast.33, s32[4,128]{1,0:T(4,128)} %bitcast.35, f32[4,128]{1,0:T(4,128)} %bitcast.37, f32[4,128]{1,0:T(4,128)} %bitcast.39, ...), custom_call_target="tpu_custom_call" | custom-call | flops 400000000 | bytes 149504 | tf_op jit(solution)/shard_map/depart/pallas_call | solution.py:47
Async XLA Ops:
  24.9 10.5 %copy-start.12 = (f32[128,128]{1,0:T(8,128)S(1)}, f32[128,128]{1,0:T(8,128)}, u32[]{:S(2)}) copy-start(f32[128,128]{1,0:T(8,128)} %get-tuple-element.21) | copy-start | bytes 196612
  24.9 10.6 %copy-start.10 = (f32[128,128]{1,0:T(8,128)S(1)}, f32[128,128]{1,0:T(8,128)}, u32[]{:S(2)}) copy-start(f32[128,128]{1,0:T(8,128)} %get-tuple-element.22) | copy-start | bytes 196612
  24.9 37.1 %all-to-all-start.1 = ((f32[64,3,128]{2,1,0:T(4,128)}), f32[64,3,128]{2,1,0:T(4,128)S(1)}, u32[]{:S(2)}, u32[]{:S(2)}) async-start(f32[64,3,128]{2,1,0:T(4,128)} %get-tuple-element.28), calls=%async_computation.1 | async-start | bytes 262144 | tf_op jit(solution)/shard_map/all_to_all | solution.py:435
  35.4 5.2 %collective-permute-start = (f32[128,128]{1,0:T(8,128)S(1)}, f32[128,128]{1,0:T(8,128)S(1)}, u32[]{:S(2)}, u32[]{:S(2)}) collective-permute-start(f32[128,128]{1,0:T(8,128)S(1)} %copy-done.12), channel_id=1, source_target_pairs={{0,64},{64,128},{128,192},{192,256},{256,320},{320,384},{384,448},... | collective-permute-start | bytes 196616 | tf_op jit(solution)/shard_map/ppermute | solution.py:393
  35.5 5.1 %collective-permute-start.1 = (f32[128,128]{1,0:T(8,128)S(1)}, f32[128,128]{1,0:T(8,128)S(1)}, u32[]{:S(2)}, u32[]{:S(2)}) collective-permute-start(f32[128,128]{1,0:T(8,128)S(1)} %copy-done.10), channel_id=1, source_target_pairs={{0,448},{64,0},{128,64},{192,128},{256,192},{320,256},{384,320},{4... | collective-permute-start | bytes 196616 | tf_op jit(solution)/shard_map/ppermute | solution.py:394
  40.6 0.6 copy-start.4
  41.2 0.6 copy-start.5
  43.6 7.0 %collective-permute-start.2 = (f32[7,16,128]{2,1,0:T(8,128)}, f32[7,16,128]{2,1,0:T(8,128)S(1)}, u32[]{:S(2)}, u32[]{:S(2)}) collective-permute-start(f32[7,16,128]{2,1,0:T(8,128)} %get-tuple-element.24), channel_id=1, source_target_pairs={{0,8},{8,16},{16,24},{24,32},{32,40},{40,48},{48,56},{56,0},{1,9},... | collective-permute-start | bytes 172040 | tf_op jit(solution)/shard_map/ppermute | solution.py:393
  48.5 7.5 %collective-permute-start.3 = (f32[7,16,128]{2,1,0:T(8,128)}, f32[7,16,128]{2,1,0:T(8,128)S(1)}, u32[]{:S(2)}, u32[]{:S(2)}) collective-permute-start(f32[7,16,128]{2,1,0:T(8,128)} %get-tuple-element.25), channel_id=1, source_target_pairs={{0,56},{8,0},{16,8},{24,16},{32,24},{40,32},{48,40},{56,48},{1,57}... | collective-permute-start | bytes 172040 | tf_op jit(solution)/shard_map/ppermute | solution.py:394
  50.6 5.4 %copy-start.6 = (f32[7,16,128]{2,1,0:T(8,128)}, f32[7,16,128]{2,1,0:T(8,128)S(1)}, u32[]{:S(2)}) copy-start(f32[7,16,128]{2,1,0:T(8,128)S(1)} %collective-permute-done.2.south) | copy-start | bytes 172036
  55.9 0.6 copy-start.7
  62.0 0.6 copy-start.1
  81.0 7.0 %copy-start.13 = (f32[128,128]{1,0:T(8,128)S(1)}, f32[128,128]{1,0:T(8,128)}, u32[]{:S(2)}) copy-start(f32[128,128]{1,0:T(8,128)} %get-tuple-element.32) | copy-start | bytes 196612
  81.0 7.1 %copy-start.11 = (f32[128,128]{1,0:T(8,128)S(1)}, f32[128,128]{1,0:T(8,128)}, u32[]{:S(2)}) copy-start(f32[128,128]{1,0:T(8,128)} %get-tuple-element.33) | copy-start | bytes 196612
  81.0 32.9 %all-to-all-start.3 = ((f32[64,4,128]{2,1,0:T(4,128)}), f32[64,4,128]{2,1,0:T(4,128)S(1)}, u32[]{:S(2)}, u32[]{:S(2)}) async-start(f32[64,4,128]{2,1,0:T(4,128)} %get-tuple-element.38), calls=%async_computation.3 | async-start | bytes 262144 | tf_op jit(solution)/shard_map/all_to_all | solution.py:458
  88.0 5.2 %collective-permute-start.4 = (f32[128,128]{1,0:T(8,128)S(1)}, f32[128,128]{1,0:T(8,128)S(1)}, u32[]{:S(2)}, u32[]{:S(2)}) collective-permute-start(f32[128,128]{1,0:T(8,128)S(1)} %copy-done.13), channel_id=1, source_target_pairs={{0,64},{64,128},{128,192},{192,256},{256,320},{320,384},{384,448},... | collective-permute-start | bytes 196616 | tf_op jit(solution)/shard_map/ppermute | solution.py:393
  88.1 5.1 %collective-permute-start.5 = (f32[128,128]{1,0:T(8,128)S(1)}, f32[128,128]{1,0:T(8,128)S(1)}, u32[]{:S(2)}, u32[]{:S(2)}) collective-permute-start(f32[128,128]{1,0:T(8,128)S(1)} %copy-done.11), channel_id=1, source_target_pairs={{0,448},{64,0},{128,64},{192,128},{256,192},{320,256},{384,320},{4... | collective-permute-start | bytes 196616 | tf_op jit(solution)/shard_map/ppermute | solution.py:394
  93.2 0.6 copy-start.2
  93.2 0.6 copy-start.3
  95.5 6.9 %collective-permute-start.6 = (f32[5,16,128]{2,1,0:T(8,128)}, f32[5,16,128]{2,1,0:T(8,128)S(1)}, u32[]{:S(2)}, u32[]{:S(2)}) collective-permute-start(f32[5,16,128]{2,1,0:T(8,128)} %get-tuple-element.35), channel_id=1, source_target_pairs={{0,8},{8,16},{16,24},{24,32},{32,40},{40,48},{48,56},{56,0},{1,9},... | collective-permute-start | bytes 122888 | tf_op jit(solution)/shard_map/ppermute | solution.py:393
  100.4 7.3 %collective-permute-start.7 = (f32[5,16,128]{2,1,0:T(8,128)}, f32[5,16,128]{2,1,0:T(8,128)S(1)}, u32[]{:S(2)}, u32[]{:S(2)}) collective-permute-start(f32[5,16,128]{2,1,0:T(8,128)} %get-tuple-element.36), channel_id=1, source_target_pairs={{0,56},{8,0},{16,8},{24,16},{32,24},{40,32},{48,40},{56,48},{1,57}... | collective-permute-start | bytes 122888 | tf_op jit(solution)/shard_map/ppermute | solution.py:394
  102.4 5.4 %copy-start.8 = (f32[5,16,128]{2,1,0:T(8,128)}, f32[5,16,128]{2,1,0:T(8,128)S(1)}, u32[]{:S(2)}) copy-start(f32[5,16,128]{2,1,0:T(8,128)S(1)} %collective-permute-done.6.south) | copy-start | bytes 122884
  107.7 0.6 copy-start.9
  114.0 0.7 copy-start

commit v2 on v1

--- a/solution.py
+++ b/solution.py
@@ -51,6 +51,7 @@
         out_specs=[vmem] * len(outs),
         scratch_shapes=list(scratch),
         cost_estimate=pl.CostEstimate(flops=flops, bytes_accessed=moved, transcendentals=0),
+        compiler_params=pltpu.CompilerParams(vmem_limit_bytes=16 << 20),
         name=body.__name__,
     )(*args)
 

time: 118 us -> 102 us (0.86)
  Pallas kernels: 27.6 us -> 14.9 us
  blocking collectives: 31.8 us -> 30 us
  local copies, waits for them, and re-layouts: 4.44 us -> 3.26 us
    pallas_call x9, Pallas kernels: 27.6 us -> 14.9 us  [call(): pl.pallas_call(body, out_shape=[jax.ShapeDtypeStruct(s, F32) for s in out...]
    all_to_all x1, blocking collectives: 13.1 us -> 11.5 us  [per_device(): found = lax.all_to_all(found, 'obs', 0, 0, tiled=True)]
    unnamed x28 -> x24, local copies, waits for them, and re-layouts: 4.44 us -> 3.26 us
  transfers between devices with their start and end apart: 10 -> 10, of which waited for: 5 -> 4; matrix products, arithmetic and copies ran while one was open for 0% -> 0% of each run, Pallas kernels for 12% -> 8%
where the time goes in v2:
time: 102 us
  starting transfers between devices  37.6 us (37%)
  blocking collectives  30 us (29%)
  waiting for transfers between devices  15 us (15%)
  Pallas kernels  14.9 us (15%)
  local copies, waits for them, and re-layouts  3.26 us (3%)
    all_to_all x1, blocking collectives, per_device(): rows = lax.all_to_all(rows, 'obs', 0, 0, tiled=True)  18.5 us
    pallas_call x9, Pallas kernels, call(): pl.pallas_call(body, out_shape=[jax.ShapeDtypeStruct(s, F32) for s in out...  14.9 us
    all_to_all x1, blocking collectives, per_device(): found = lax.all_to_all(found, 'obs', 0, 0, tiled=True)  11.5 us
    ppermute x4, waiting for transfers between devices, pair(): lax.ppermute(back, axis, ring(axis, -1))  10.5 us
    all_to_all x1, starting transfers between devices, per_device(): table = lax.all_to_all(table, ('gx', 'gy'), 0, 0, tiled=True)  10.5 us
    ppermute x4, starting transfers between devices, pair(): lax.ppermute(forward, axis, ring(axis, 1))  10.1 us
    ppermute x4, starting transfers between devices, pair(): lax.ppermute(back, axis, ring(axis, -1))  9.51 us
    all_to_all x1, starting transfers between devices, per_device(): columns = lax.all_to_all(columns, ('gx', 'gy'), 0, 0, tiled=True)  7.54 us
  transfers between devices with their start and end apart: 10, of which 4 were waited for; matrix products, arithmetic and copies ran while one was open for 0% of the time, Pallas kernels for 8%

profile of v2, /device:TPU:24, one launch (start us, length us, event | category | flops | bytes accessed | tf_op | source)
XLA Modules:
  0.0 101.6 jit_solution(14595758635111164974)
XLA Ops:
  0.6 0.0 copy-start.9
  0.6 0.0 copy-start.8
  0.7 0.0 copy-start.7
  0.7 0.0 copy-start.6
  0.7 0.0 copy-start.5
  0.7 0.0 copy-start.4
  0.7 0.6 copy-done.9
  1.3 0.0 copy-done.8
  1.3 0.0 copy-done.7
  1.3 0.0 copy-done.6
  1.4 0.0 copy-done.5
  1.4 0.0 copy-done.4
  1.4 0.0 copy-start
  1.4 0.9 copy-done
  2.3 0.0 copy-start.2
  2.3 0.9 copy-done.2
  3.2 0.2 pack_inputs.1
  3.5 0.0 copy-start.11
  3.5 18.5 %all_to_all.32 = f32[8,16,128]{2,1,0:T(8,128)S(1)} all-to-all(f32[8,16,128]{2,1,0:T(8,128)S(1)} %bitcast.27), channel_id=1, replica_groups=mesh['gx'=8,'gy'=8,'obs'=8] {'obs'}, dimensions={0} | all-to-all | bytes 131072 | tf_op jit(solution)/shard_map/all_to_all | solution.py:428
  22.0 0.0 copy-start.10
  22.0 0.0 copy-done.11
  22.0 0.7 copy-done.10
  22.7 0.0 copy-start.3
  22.7 2.6 %tables.1 = (f32[64,3,128]{2,1,0:T(4,128)}, f32[1,512]{1,0:T(1,128)S(1)}) custom-call(f32[128,128]{1,0:T(8,128)S(1)} %bitcast.28, s32[1,512]{1,0:T(1,128)S(1)} %bitcast.42, s32[1,512]{1,0:T(1,128)S(1)} %bitcast.41), custom_call_target="tpu_custom_call" | custom-call | flops 400000000 | bytes 169984 | tf_op jit(solution)/shard_map/tables/pallas_call | solution.py:47
  25.3 0.0 copy-start.1
  25.3 10.5 %all-to-all-start.1 = ((f32[64,3,128]{2,1,0:T(4,128)}), f32[64,3,128]{2,1,0:T(4,128)S(1)}, u32[]{:S(2)}, u32[]{:S(2)}) async-start(f32[64,3,128]{2,1,0:T(4,128)} %get-tuple-element.28), calls=%async_computation.1 | async-start | bytes 262144 | tf_op jit(solution)/shard_map/all_to_all | solution.py:436
  35.8 0.1 collective-permute-start
  35.9 2.8 %collective-permute-start.1 = (f32[128,128]{1,0:T(8,128)S(1)}, f32[128,128]{1,0:T(8,128)S(1)}, u32[]{:S(2)}, u32[]{:S(2)}) collective-permute-start(f32[128,128]{1,0:T(8,128)S(1)} %get-tuple-element.22), channel_id=1, source_target_pairs={{0,448},{64,0},{128,64},{192,128},{256,192},{320,256},{384,320},{4... | collective-permute-start | bytes 196616 | tf_op jit(solution)/shard_map/ppermute | solution.py:395
  38.7 2.3 %collective-permute-done.left = f32[128,128]{1,0:T(8,128)S(1)} collective-permute-done((f32[128,128]{1,0:T(8,128)S(1)}, f32[128,128]{1,0:T(8,128)S(1)}, u32[]{:S(2)}, u32[]{:S(2)}) %collective-permute-start) | collective-permute-done | bytes 65568 | tf_op jit(solution)/shard_map/ppermute | solution.py:394
  41.0 0.0 collective-permute-done.1.right
  41.0 0.0 copy-done.3
  41.0 0.0 copy-done.1
  41.0 4.9 %collective-permute-start.2 = (f32[7,16,128]{2,1,0:T(8,128)S(1)}, f32[7,16,128]{2,1,0:T(8,128)S(1)}, u32[]{:S(2)}, u32[]{:S(2)}) collective-permute-start(f32[7,16,128]{2,1,0:T(8,128)S(1)} %get-tuple-element.24), channel_id=1, source_target_pairs={{0,8},{8,16},{16,24},{24,32},{32,40},{40,48},{48,56},{56,0},{1,9},... | collective-permute-start | bytes 172040 | tf_op jit(solution)/shard_map/ppermute | solution.py:394
  45.9 1.9 %collective-permute-start.3 = (f32[7,16,128]{2,1,0:T(8,128)S(1)}, f32[7,16,128]{2,1,0:T(8,128)S(1)}, u32[]{:S(2)}, u32[]{:S(2)}) collective-permute-start(f32[7,16,128]{2,1,0:T(8,128)S(1)} %get-tuple-element.25), channel_id=1, source_target_pairs={{0,56},{8,0},{16,8},{24,16},{32,24},{40,32},{48,40},{56,48},{1,57}... | collective-permute-start | bytes 172040 | tf_op jit(solution)/shard_map/ppermute | solution.py:395
  47.9 0.0 collective-permute-done.2.south
  47.9 5.3 %collective-permute-done.3.north = f32[7,16,128]{2,1,0:T(8,128)S(1)} collective-permute-done((f32[7,16,128]{2,1,0:T(8,128)S(1)}, f32[7,16,128]{2,1,0:T(8,128)S(1)}, u32[]{:S(2)}, u32[]{:S(2)}) %collective-permute-start.3) | collective-permute-done | bytes 57376 | tf_op jit(solution)/shard_map/ppermute | solution.py:395
  53.2 3.7 %diffuse_control.1 = (f32[4,128,128]{2,1,0:T(8,128)S(1)}, f32[10,160,128]{2,1,0:T(8,128)S(1)}) custom-call(f32[4,128,128]{2,1,0:T(8,128)S(1)} %bitcast.20, f32[2,128,128]{2,1,0:T(8,128)S(1)} %bitcast.24, f32[128,128]{1,0:T(8,128)S(1)} %get-tuple-element.23.strip, f32[7,16,128]{2,1,0:T(8,128)S(1)} %collective-permute-done.2.south, ...), custom_call_target="tpu_custom_call" | custom-call | flops 40000000 | bytes 1654784 | tf_op jit(solution)/shard_map/diffuse_control/pallas_call | solution.py:47
  56.9 0.0 all-to-all-done.1.sent
  56.9 0.9 gather.1
  57.8 11.5 %all_to_all.33 = f32[8,32,128]{2,1,0:T(8,128)S(1)} all-to-all(f32[8,32,128]{2,1,0:T(8,128)S(1)} %bitcast.26), channel_id=1, replica_groups=mesh['gx'=8,'gy'=8,'obs'=8] {'obs'}, dimensions={0} | all-to-all | bytes 262144 | tf_op jit(solution)/shard_map/all_to_all | solution.py:451
  69.2 1.8 %scatter.1 = (f32[4,128,128]{2,1,0:T(8,128)S(1)}, f32[128,128]{1,0:T(8,128)S(1)}, f32[128,128]{1,0:T(8,128)S(1)}, f32[64,4,128]{2,1,0:T(4,128)}) custom-call(f32[256,128]{1,0:T(8,128)S(1)} %bitcast.25, f32[136,128]{1,0:T(8,128)S(1)} %get-tuple-element.30.tab), custom_call_target="tpu_custom_call" | custom-call | flops 400000000 | bytes 724992 | tf_op jit(solution)/shard_map/scatter/pallas_call | solution.py:47
  71.1 7.5 %all-to-all-start.3 = ((f32[64,4,128]{2,1,0:T(4,128)}), f32[64,4,128]{2,1,0:T(4,128)S(1)}, u32[]{:S(2)}, u32[]{:S(2)}) async-start(f32[64,4,128]{2,1,0:T(4,128)} %get-tuple-element.38), calls=%async_computation.3 | async-start | bytes 262144 | tf_op jit(solution)/shard_map/all_to_all | solution.py:459
  78.6 0.1 collective-permute-start.4
  78.8 2.8 %collective-permute-start.5 = (f32[128,128]{1,0:T(8,128)S(1)}, f32[128,128]{1,0:T(8,128)S(1)}, u32[]{:S(2)}, u32[]{:S(2)}) collective-permute-start(f32[128,128]{1,0:T(8,128)S(1)} %get-tuple-element.33), channel_id=1, source_target_pairs={{0,448},{64,0},{128,64},{192,128},{256,192},{320,256},{384,320},{4... | collective-permute-start | bytes 196616 | tf_op jit(solution)/shard_map/ppermute | solution.py:395
  81.6 2.3 %collective-permute-done.4.left = f32[128,128]{1,0:T(8,128)S(1)} collective-permute-done((f32[128,128]{1,0:T(8,128)S(1)}, f32[128,128]{1,0:T(8,128)S(1)}, u32[]{:S(2)}, u32[]{:S(2)}) %collective-permute-start.4) | collective-permute-done | bytes 65568 | tf_op jit(solution)/shard_map/ppermute | solution.py:394
  83.8 0.0 collective-permute-done.5.right
  83.9 4.9 %collective-permute-start.6 = (f32[5,16,128]{2,1,0:T(8,128)S(1)}, f32[5,16,128]{2,1,0:T(8,128)S(1)}, u32[]{:S(2)}, u32[]{:S(2)}) collective-permute-start(f32[5,16,128]{2,1,0:T(8,128)S(1)} %get-tuple-element.35), channel_id=1, source_target_pairs={{0,8},{8,16},{16,24},{24,32},{32,40},{40,48},{48,56},{56,0},{1,9},... | collective-permute-start | bytes 122888 | tf_op jit(solution)/shard_map/ppermute | solution.py:394
  88.8 1.9 %collective-permute-start.7 = (f32[5,16,128]{2,1,0:T(8,128)S(1)}, f32[5,16,128]{2,1,0:T(8,128)S(1)}, u32[]{:S(2)}, u32[]{:S(2)}) collective-permute-start(f32[5,16,128]{2,1,0:T(8,128)S(1)} %get-tuple-element.36), channel_id=1, source_target_pairs={{0,56},{8,0},{16,8},{24,16},{32,24},{40,32},{48,40},{56,48},{1,57}... | collective-permute-start | bytes 122888 | tf_op jit(solution)/shard_map/ppermute | solution.py:395
  90.7 0.0 collective-permute-done.6.south
  90.7 5.2 %collective-permute-done.7.north = f32[5,16,128]{2,1,0:T(8,128)S(1)} collective-permute-done((f32[5,16,128]{2,1,0:T(8,128)S(1)}, f32[5,16,128]{2,1,0:T(8,128)S(1)}, u32[]{:S(2)}, u32[]{:S(2)}) %collective-permute-start.7) | collective-permute-done | bytes 40992 | tf_op jit(solution)/shard_map/ppermute | solution.py:395
  95.9 4.2 %diffuse_pulled.1 = f32[4,128,128]{2,1,0:T(8,128)} custom-call(f32[4,128,128]{2,1,0:T(8,128)S(1)} %get-tuple-element.31.pulled, f32[128,128]{1,0:T(8,128)S(1)} %get-tuple-element.34.strip, f32[5,16,128]{2,1,0:T(8,128)S(1)} %collective-permute-done.6.south, f32[5,16,128]{2,1,0:T(8,128)S(1)} %collective-permute-done.7.north, ...), custom_call_target="tpu_custom_call" | custom-call | flops 40000000 | bytes 1753088 | tf_op jit(solution)/shard_map/diffuse_pulled/pallas_call | solution.py:47
  100.1 0.0 all-to-all-done.3.columns
  100.1 1.4 %depart.1 = f32[4,128]{1,0:T(4,128)} custom-call(f32[64,4,128]{2,1,0:T(4,128)S(1)} %all-to-all-done.3.columns, s32[1,512]{1,0:T(1,128)S(1)} %bitcast.43, f32[1,512]{1,0:T(1,128)S(1)} %get-tuple-element.39.slots, s32[4,128]{1,0:T(4,128)S(1)} %bitcast.30, s32[4,128]{1,0:T(4,128)S(1)} %bitcast.32, s32[4,128]{1,0:T(4,128)S(1)} %bitcast.34, ...), custom_call_target="tpu_custom_call" | custom-call | flops 400000000 | bytes 149504 | tf_op jit(solution)/shard_map/depart/pallas_call | solution.py:47
  (2 shorter events, 0.0 us)
Async XLA Ops:
  0.6 0.7 copy-start.9
  0.6 0.7 copy-start.8
  0.7 0.7 copy-start.7
  0.7 0.7 copy-start.6
  0.7 0.7 copy-start.5
  0.7 0.7 copy-start.4
  1.4 0.9 copy-start
  2.3 0.9 copy-start.2
  3.5 18.5 %copy-start.11 = (s32[512,1]{0,1:T(1,128)S(1)}, s32[512,1]{0,1:T(1,128)}, u32[]{:S(2)}) copy-start(s32[512,1]{0,1:T(1,128)} %param.12) | copy-start | bytes 6148
  22.0 0.7 copy-start.10
  22.7 18.3 %copy-start.3 = (f32[2,1,128,128]{3,2,1,0:T(8,128)S(1)}, f32[2,1,128,128]{3,2,1,0:T(8,128)}, u32[]{:S(2)}) copy-start(f32[2,1,128,128]{3,2,1,0:T(8,128)} %param.11) | copy-start | bytes 393220
  25.3 15.7 %copy-start.1 = (f32[4,1,128,128]{3,2,1,0:T(8,128)S(1)}, f32[4,1,128,128]{3,2,1,0:T(8,128)}, u32[]{:S(2)}) copy-start(f32[4,1,128,128]{3,2,1,0:T(8,128)} %param.10) | copy-start | bytes 786436
  25.3 31.6 %all-to-all-start.1 = ((f32[64,3,128]{2,1,0:T(4,128)}), f32[64,3,128]{2,1,0:T(4,128)S(1)}, u32[]{:S(2)}, u32[]{:S(2)}) async-start(f32[64,3,128]{2,1,0:T(4,128)} %get-tuple-element.28), calls=%async_computation.1 | async-start | bytes 262144 | tf_op jit(solution)/shard_map/all_to_all | solution.py:436
  35.8 5.2 %collective-permute-start = (f32[128,128]{1,0:T(8,128)S(1)}, f32[128,128]{1,0:T(8,128)S(1)}, u32[]{:S(2)}, u32[]{:S(2)}) collective-permute-start(f32[128,128]{1,0:T(8,128)S(1)} %get-tuple-element.21), channel_id=1, source_target_pairs={{0,64},{64,128},{128,192},{192,256},{256,320},{320,384},{384,448},... | collective-permute-start | bytes 196616 | tf_op jit(solution)/shard_map/ppermute | solution.py:394
  35.9 5.1 %collective-permute-start.1 = (f32[128,128]{1,0:T(8,128)S(1)}, f32[128,128]{1,0:T(8,128)S(1)}, u32[]{:S(2)}, u32[]{:S(2)}) collective-permute-start(f32[128,128]{1,0:T(8,128)S(1)} %get-tuple-element.22), channel_id=1, source_target_pairs={{0,448},{64,0},{128,64},{192,128},{256,192},{320,256},{384,320},{4... | collective-permute-start | bytes 196616 | tf_op jit(solution)/shard_map/ppermute | solution.py:395
  41.0 6.8 %collective-permute-start.2 = (f32[7,16,128]{2,1,0:T(8,128)S(1)}, f32[7,16,128]{2,1,0:T(8,128)S(1)}, u32[]{:S(2)}, u32[]{:S(2)}) collective-permute-start(f32[7,16,128]{2,1,0:T(8,128)S(1)} %get-tuple-element.24), channel_id=1, source_target_pairs={{0,8},{8,16},{16,24},{24,32},{32,40},{40,48},{48,56},{56,0},{1,9},... | collective-permute-start | bytes 172040 | tf_op jit(solution)/shard_map/ppermute | solution.py:394
  45.9 7.3 %collective-permute-start.3 = (f32[7,16,128]{2,1,0:T(8,128)S(1)}, f32[7,16,128]{2,1,0:T(8,128)S(1)}, u32[]{:S(2)}, u32[]{:S(2)}) collective-permute-start(f32[7,16,128]{2,1,0:T(8,128)S(1)} %get-tuple-element.25), channel_id=1, source_target_pairs={{0,56},{8,0},{16,8},{24,16},{32,24},{40,32},{48,40},{56,48},{1,57}... | collective-permute-start | bytes 172040 | tf_op jit(solution)/shard_map/ppermute | solution.py:395
  71.1 29.1 %all-to-all-start.3 = ((f32[64,4,128]{2,1,0:T(4,128)}), f32[64,4,128]{2,1,0:T(4,128)S(1)}, u32[]{:S(2)}, u32[]{:S(2)}) async-start(f32[64,4,128]{2,1,0:T(4,128)} %get-tuple-element.38), calls=%async_computation.3 | async-start | bytes 262144 | tf_op jit(solution)/shard_map/all_to_all | solution.py:459
  78.6 5.2 %collective-permute-start.4 = (f32[128,128]{1,0:T(8,128)S(1)}, f32[128,128]{1,0:T(8,128)S(1)}, u32[]{:S(2)}, u32[]{:S(2)}) collective-permute-start(f32[128,128]{1,0:T(8,128)S(1)} %get-tuple-element.32), channel_id=1, source_target_pairs={{0,64},{64,128},{128,192},{192,256},{256,320},{320,384},{384,448},... | collective-permute-start | bytes 196616 | tf_op jit(solution)/shard_map/ppermute | solution.py:394
  78.8 5.1 %collective-permute-start.5 = (f32[128,128]{1,0:T(8,128)S(1)}, f32[128,128]{1,0:T(8,128)S(1)}, u32[]{:S(2)}, u32[]{:S(2)}) collective-permute-start(f32[128,128]{1,0:T(8,128)S(1)} %get-tuple-element.33), channel_id=1, source_target_pairs={{0,448},{64,0},{128,64},{192,128},{256,192},{320,256},{384,320},{4... | collective-permute-start | bytes 196616 | tf_op jit(solution)/shard_map/ppermute | solution.py:395
  83.9 6.8 %collective-permute-start.6 = (f32[5,16,128]{2,1,0:T(8,128)S(1)}, f32[5,16,128]{2,1,0:T(8,128)S(1)}, u32[]{:S(2)}, u32[]{:S(2)}) collective-permute-start(f32[5,16,128]{2,1,0:T(8,128)S(1)} %get-tuple-element.35), channel_id=1, source_target_pairs={{0,8},{8,16},{16,24},{24,32},{32,40},{40,48},{48,56},{56,0},{1,9},... | collective-permute-start | bytes 122888 | tf_op jit(solution)/shard_map/ppermute | solution.py:394
  88.8 7.1 %collective-permute-start.7 = (f32[5,16,128]{2,1,0:T(8,128)S(1)}, f32[5,16,128]{2,1,0:T(8,128)S(1)}, u32[]{:S(2)}, u32[]{:S(2)}) collective-permute-start(f32[5,16,128]{2,1,0:T(8,128)S(1)} %get-tuple-element.36), channel_id=1, source_target_pairs={{0,56},{8,0},{16,8},{24,16},{32,24},{40,32},{48,40},{56,48},{1,57}... | collective-permute-start | bytes 122888 | tf_op jit(solution)/shard_map/ppermute | solution.py:395
